TPU v7x, 32 devices: a whole 2x2x4 slice. The times are simulated.
32 devices in a mesh: dp: 16 (over z, y, x), chan: 2 (over core).
Axes of the slice: x: 2, y: 2, z: 4, core: 2. Of those that a mesh axis runs over, the one named last changes fastest.
Arguments:
- pixels: bfloat16 [32, 1024, 512], P('dp', None, 'chan'), may hold values from -6 to 6
- tile_ids: int32 [32, 1024], P('dp'), may hold values from 0 to 3, as said below
- first_gain: float32 [512], P('chan'), may hold values from 0.1 to 1.9
- first_shift: float32 [512], P('chan'), may hold values from -3 to 3
- first_conv: bfloat16 [9, 512, 512], P(None, None, 'chan'), may hold values from -0.09375 to 0.09375
- first_bias: float32 [512], P('chan'), may hold values from -3 to 3
- second_gain: float32 [512], P('chan'), may hold values from 0.1 to 1.9
- second_shift: float32 [512], P('chan'), may hold values from -3 to 3
- second_conv: bfloat16 [9, 512, 512], P(None, 'chan'), may hold values from -0.125 to 0.125
- second_bias: float32 [512], P('chan'), may hold values from -3 to 3
- attn_gain: float32 [512], P('chan'), may hold values from 0.1 to 1.9
- attn_shift: float32 [512], P('chan'), may hold values from -3 to 3
- query_weight: bfloat16 [512, 512], P(None, 'chan'), may hold values from -0.375 to 0.375
- query_bias: float32 [512], P('chan'), may hold values from -3 to 3
- key_weight: bfloat16 [512, 512], P(None, 'chan'), may hold values from -0.375 to 0.375
- value_weight: bfloat16 [512, 512], P(None, 'chan'), may hold values from -0.25 to 0.25
- value_bias: float32 [512], P('chan'), may hold values from -3 to 3
- proj_weight: bfloat16 [512, 512], P('chan'), may hold values from -0.5 to 0.5
- proj_bias: float32 [512], P('chan'), may hold values from -3 to 3
- cotangent: bfloat16 [32, 1024, 512], P('dp', None, 'chan'), may hold values from -6 to 6
Outputs:
- block_out: float32 [32, 1024, 512], P('dp', None, 'chan')
- pixel_grad: float32 [32, 1024, 512], P('dp', None, 'chan')
- grad_first_gain: float32 [512], P('chan')
- grad_first_shift: float32 [512], P('chan')
- grad_first_conv: float32 [9, 512, 512], P(None, None, 'chan')
- grad_first_bias: float32 [512], P('chan')
- grad_second_gain: float32 [512], P('chan')
- grad_second_shift: float32 [512], P('chan')
- grad_second_conv: float32 [9, 512, 512], P(None, 'chan')
- grad_second_bias: float32 [512], P('chan')
- grad_attn_gain: float32 [512], P('chan')
- grad_attn_shift: float32 [512], P('chan')
- grad_query_weight: float32 [512, 512], P(None, 'chan')
- grad_query_bias: float32 [512], P('chan')
- grad_key_weight: float32 [512, 512], P(None, 'chan')
- grad_value_weight: float32 [512, 512], P(None, 'chan')
- grad_value_bias: float32 [512], P('chan')
- grad_proj_weight: float32 [512, 512], P('chan')
- grad_proj_bias: float32 [512], P('chan')
Inputs may be any that keep to these rules, and one draw needn't show every extreme that they name: `tile_ids`: constant over each aligned 16 x 16 tile of a canvas; the pixels of one canvas with equal ids form one image.
All inputs are finite; a program needn't handle non-finite values.
Results may differ from a plain program's by a relative error of at most 0.024.
Values may be sent and summed in bfloat16 or wider, within the bound.
No kernel may reach another device: no remote copies, remote signals or barrier semaphores. Data moves between devices by JAX's collectives and lax.ppermute only.
A program may use at most 192 MiB of HBM per device.

v0:
```python
import functools
import math
import jax
import jax.numpy as jnp
from jax import lax
from jax.experimental import pallas as pl
from jax.experimental.pallas import tpu as pltpu
from jax.sharding import PartitionSpec as P

C = 512
HALF = 256
GROUP = 16
SIDE = 32
PIX = 1024
EPSILON = 1e-06
BF = jnp.bfloat16
F32 = jnp.float32
MB = 1024 * 1024
VM = pl.BlockSpec(memory_space=pltpu.VMEM)
SM = pl.BlockSpec(memory_space=pltpu.SMEM)
HBM = pl.BlockSpec(memory_space=pltpu.HBM)
SCALE = C ** (-0.5)
LOG2E = 1.4426950408889634


def dot(first, second):
    return jnp.dot(first, second, preferred_element_type=F32)


def dot_nt(first, second):
    return lax.dot_general(first, second, (((1,), (1,)), ((), ())), preferred_element_type=F32)


def dot_tn(first, second):
    return lax.dot_general(first, second, (((0,), (0,)), ((), ())), preferred_element_type=F32)


def at_row(row):
    return pl.ds(pl.multiple_of(row * SIDE, SIDE), SIDE)


def group_sums(rows):
    full = jnp.concatenate(rows, 0)
    width = full.shape[1]
    lane = lax.broadcasted_iota(jnp.int32, full.shape, 1)
    for step in (1, 2, 4, 8):
        full = full + jnp.where(
            (lane & step) == 0, pltpu.roll(full, width - step, 1), pltpu.roll(full, step, 1)
        )
    return [full[i : i + 1] for i in range(len(rows))]


def image_means(sums, eq_ref):
    rows = []
    for i in range(4):
        total, count = 0.0, 0.0
        for j in range(4):
            total = total + eq_ref[4 * i + j] * sums[j]
            count = count + eq_ref[4 * i + j]
        rows.append(total / (count * float(256 * GROUP)))
    return group_sums(rows)


def tiles_of(rows):
    return rows.reshape(2, 16, rows.shape[-1])


def pair(rows, top):
    return jnp.concatenate([rows[2 * top + side].reshape(1, 1, -1) for side in range(2)], 0)


def over_canvas(step, count, width=C, unroll=2):
    found = [[] for _ in range(count)]
    for top in range(2):
        zero = tuple(jnp.zeros((2, 16, width), F32) for _ in range(count))

        def body(index, carry, top=top):
            return tuple(a + b for a, b in zip(carry, step(top, top * 16 + index)))

        totals = lax.fori_loop(0, 16, body, zero, unroll=unroll)
        for n in range(count):
            columns = jnp.sum(totals[n], axis=1)
            found[n] += [columns[0:1], columns[1:2]]
    return found


def for_rows(step, unroll=2):
    for top in range(2):

        def body(index, carry, top=top):
            step(top, top * 16 + index)
            return carry

        lax.fori_loop(0, 16, body, 0, unroll=unroll)


def norm_stats(load, eq_ref, width):
    (sums,) = over_canvas(lambda top, row: (tiles_of(load(row)),), 1, width)
    means = image_means(sums, eq_ref)
    centers = [pair(means, top) for top in range(2)]

    def square(top, row):
        off = tiles_of(load(row)) - centers[top]
        return (off * off,)

    (squares,) = over_canvas(square, 1, width)
    rstds = [lax.rsqrt(v + EPSILON) for v in image_means(squares, eq_ref)]
    return means, rstds


def swish(value):
    half = 0.5 * value
    return half + half * jnp.tanh(half)


def norm_forward(load, out_refs, stat_ref, eq_ref, gain, shift, act):
    width = gain.shape[-1]
    means, rstds = norm_stats(load, eq_ref, width)
    stat_ref[...] = jnp.concatenate(means + rstds, 0)
    centers = [pair(means, top) for top in range(2)]
    slopes = [pair([r * gain for r in rstds], top) for top in range(2)]
    offset = shift.reshape(1, 1, width)

    def step(top, row):
        value = (tiles_of(load(row)) - centers[top]) * slopes[top] + offset
        value = act(value).reshape(SIDE, width).astype(BF)
        held = width // len(out_refs)
        for index, ref in enumerate(out_refs):
            ref[at_row(row), :] = value[:, index * held : (index + 1) * held]

    for_rows(step)


def norm_backward(load, load_grad, keep_ref, stat_ref, eq_ref, gain, shift, with_swish, finish):
    stats = stat_ref[...]
    means = [stats[i : i + 1] for i in range(4)]
    rstds = [stats[4 + i : 5 + i] for i in range(4)]
    centers = [pair(means, top) for top in range(2)]
    rates = [pair(rstds, top) for top in range(2)]
    scale, offset = gain.reshape(1, 1, C), shift.reshape(1, 1, C)

    def first(top, row):
        unit = (tiles_of(load(row)) - centers[top]) * rates[top]
        grad = tiles_of(load_grad(row))
        if with_swish:
            value = unit * scale + offset
            gate = 0.5 + 0.5 * jnp.tanh(0.5 * value)
            grad = grad * (gate * (1.0 + value * (1.0 - gate)))
            keep_ref[at_row(row), :] = grad.reshape(SIDE, C)
        return grad, grad * unit

    plain, scaled = over_canvas(first, 2)
    mean_plain = image_means([p * gain for p in plain], eq_ref)
    mean_scaled = image_means([s * gain for s in scaled], eq_ref)
    first_means = [pair(mean_plain, top) for top in range(2)]
    second_means = [pair(mean_scaled, top) for top in range(2)]

    def second(top, row):
        unit = (tiles_of(load(row)) - centers[top]) * rates[top]
        grad = tiles_of(keep_ref[at_row(row), :] if with_swish else load_grad(row))
        change = rates[top] * (grad * scale - first_means[top] - unit * second_means[top])
        finish(row, change.reshape(SIDE, C))

    for_rows(second)
    return sum(scaled), sum(plain)


BAND = PIX // 2 + 2 * SIDE


def row_mask(eq_ref, target, source, right):
    column = lax.broadcasted_iota(jnp.int32, (SIDE, 128), 0)

    def eq(side, other):
        return eq_ref[(2 * target + side) * 4 + 2 * source + other]

    if right == 0:
        mask = jnp.where(column < 16, eq(0, 0), eq(1, 1))
    elif right < 0:
        mask = jnp.where(column < 16, eq(0, 0), jnp.where(column == 16, eq(1, 0), eq(1, 1)))
        mask = jnp.where(column == 0, 0.0, mask)
    else:
        mask = jnp.where(column < 15, eq(0, 0), jnp.where(column == 15, eq(0, 1), eq(1, 1)))
        mask = jnp.where(column == SIDE - 1, 0.0, mask)
    return mask.astype(BF)


def fill_bands(band_ref, load, eq_ref, columns=None):
    width = band_ref.shape[2] // 3

    def put(half, place, value, masks):
        moved = [pltpu.roll(value, 1, 0), value, pltpu.roll(value, SIDE - 1, 0)]
        for index in range(3):
            part = moved[index].astype(BF)
            if masks[index] is not None:
                part = part * jnp.concatenate([masks[index]] * (width // 128), 1)
            if columns is None:
                band_ref[half, at_row(place), index * width : (index + 1) * width] = part
            else:
                for number in range(width // HALF):
                    where = pl.ds(columns(index, number), HALF)
                    band_ref[half, at_row(place), where] = part[
                        :, number * HALF : (number + 1) * HALF]

    for half in range(2):
        inner = [row_mask(eq_ref, half, half, -1), None, row_mask(eq_ref, half, half, 1)]

        def body(index, carry, half=half, inner=inner):
            put(half, index + 1, load(half * 16 + index).astype(F32), inner)
            return carry

        lax.fori_loop(0, 16, body, 0, unroll=2)
        across = [row_mask(eq_ref, half, 1 - half, right) for right in (-1, 0, 1)]
        put(half, 17 - 17 * half, load(16 - half).astype(F32), across)
        band_ref[half, 17 * half * SIDE : (17 * half + 1) * SIDE, :] = jnp.zeros(
            (SIDE, 3 * width), BF)


def half_rows(half):
    return pl.ds(pl.multiple_of(half * (PIX // 2), PIX // 2), PIX // 2)


def tap_band(band_ref, half, down):
    if isinstance(down, int):
        return band_ref[half, down * SIDE : down * SIDE + PIX // 2, :]
    return band_ref[half, pl.ds(pl.multiple_of(down * SIDE, SIDE), PIX // 2), :]


def parts_apart(index, number):
    return number * 3 * HALF + index * HALF


def swapped(core, number):
    return pl.multiple_of((core ^ number) * HALF, HALF)


def start_all(copies):
    for copy in copies:
        copy.start()
    return copies


def wait_all(copies):
    for copy in copies:
        copy.wait()


def half_copies(core, source, target, sems):
    return [start_all([
        pltpu.make_async_copy(source.at[pl.ds(3 * group, 3), pl.ds(swapped(core, part), HALF), :],
                              target.at[group, part], sems.at[group, part])
        for part in range(2)]) for group in range(3)]


def half_conv(band, weight, copies, bias, total):
    for down in range(3):
        wait_all(copies[down])

        def body(half, carry, down=down):
            at = half_rows(half)
            value = dot(tap_band(band, half, down), weight[down].reshape(6 * HALF, HALF))
            total[at, :] = value + (total[at, :] if down > 0 else bias)
            return carry

        lax.fori_loop(0, 2, body, 0)


def tap_copies(core, own_ref, peer_ref, all_ref, sems, group):
    lead = (pl.ds(3 * group, 3),)
    return weight_copies(core, own_ref, peer_ref, all_ref, sems.at[group], lead)


def weight_copies(core, own_ref, peer_ref, all_ref, sems, lead):
    copies = []
    for local in range(2):
        source = pl.ds(pl.multiple_of((core ^ local) * HALF, HALF), HALF)
        target = pl.ds(local * HALF, HALF)
        for which, ref in enumerate((own_ref, peer_ref)):
            held = pl.ds(which * HALF, HALF)
            if own_ref.shape[-1] == HALF:
                src, dst = (source, slice(None)), (target, held)
            else:
                src, dst = (slice(None), source), (held, target)
            copies.append(
                pltpu.make_async_copy(
                    ref.at[lead + src], all_ref.at[lead + dst], sems.at[2 * local + which]
                )
            )
    return copies


def params(limit):
    return pltpu.CompilerParams(vmem_limit_bytes=limit * MB)


def cost(micros):
    return pl.CostEstimate(flops=int(micros * 1.1e9), bytes_accessed=1 << 20, transcendentals=0)


def shape(rows, columns, dtype):
    return jax.ShapeDtypeStruct((rows, columns), dtype)


def in_hbm(*arrays):
    return [pltpu.with_memory_space_constraint(array, pltpu.HBM) for array in arrays]


def fetch(source, target, sem):
    copy = pltpu.make_async_copy(source, target, sem)
    copy.start()
    return copy


def both_rows(own_ref, peer_ref, row):
    return jnp.concatenate([own_ref[at_row(row), :], peer_ref[at_row(row), :]], 1).astype(F32)


def front_kernel(core_ref, eq_ref, x_hbm, xp_hbm, w_hbm, vec_ref, peer_ref, act_own_hbm, act_peer_hbm, stat_own, stat_peer, band,
                 conv_hbm, next_ref, stat2_ref, x_own, x_peer, act_own, act_peer, weight, total, sems):
    core = core_ref[0]
    first = fetch(x_hbm.at[core], x_own, sems.at[3, 0])
    second = fetch(xp_hbm.at[core], x_peer, sems.at[3, 1])
    copies = half_copies(core, w_hbm, weight, sems)
    first.wait()
    norm_forward(lambda row: x_own[at_row(row), :].astype(F32), (act_own,), stat_own, eq_ref,
                 vec_ref[0:1, :], vec_ref[1:2, :], swish)
    second.wait()
    norm_forward(lambda row: x_peer[at_row(row), :].astype(F32), (act_peer,), stat_peer, eq_ref,
                 peer_ref[0:1, :], peer_ref[1:2, :], swish)
    stores = [fetch(act_own, act_own_hbm, sems.at[4, 0]), fetch(act_peer, act_peer_hbm, sems.at[4, 1])]
    fill_bands(band, lambda row: both_rows(act_own, act_peer, row), eq_ref, parts_apart)
    half_conv(band, weight, copies, vec_ref[2:3, :], total)
    stores.append(fetch(total, conv_hbm, sems.at[3, 0]))
    norm_forward(lambda row: total[at_row(row), :], (next_ref,), stat2_ref, eq_ref, vec_ref[3:4, :],
                 vec_ref[4:5, :], swish)
    wait_all(stores)


def front_peer_kernel(core_ref, eq_ref, band, w_hbm, vec_ref, conv_hbm, next_ref, stat2_ref, weight,
                      total, sems):
    copies = half_copies(core_ref[0], w_hbm, weight, sems)
    half_conv(band, weight, copies, vec_ref[2:3, :], total)
    store = fetch(total, conv_hbm, sems.at[3, 0])
    norm_forward(lambda row: total[at_row(row), :], (next_ref,), stat2_ref, eq_ref, vec_ref[3:4, :],
                 vec_ref[4:5, :], swish)
    store.wait()


def front_call(core, eq, pixels, pixels_peer, weight, own_vectors, peer_vectors):
    half = pltpu.HBM((PIX, HALF), BF)
    return pl.pallas_call(
        front_kernel,
        out_shape=(half, half, shape(8, HALF, F32), shape(8, HALF, F32),
                   pltpu.VMEM((2, BAND, 3 * C), BF), pltpu.HBM((PIX, HALF), F32),
                   shape(PIX, HALF, BF), shape(8, HALF, F32)),
        in_specs=[SM, SM, HBM, HBM, HBM, VM, VM],
        out_specs=(HBM, HBM, VM, VM, VM, HBM, VM, VM),
        scratch_shapes=[pltpu.VMEM((PIX, HALF), BF)] * 4
        + [pltpu.VMEM((3, 2, 3, HALF, HALF), BF), pltpu.VMEM((PIX, HALF), F32),
           pltpu.SemaphoreType.DMA((5, 2))],
        name="front", compiler_params=params(14), cost_estimate=cost(9),
    )(core, eq, *in_hbm(pixels, pixels_peer, weight), own_vectors, peer_vectors)


def front_peer_call(core, eq, band, weight, vec):
    return pl.pallas_call(
        front_peer_kernel,
        out_shape=(pltpu.HBM((PIX, HALF), F32), shape(PIX, HALF, BF), shape(8, HALF, F32)),
        in_specs=[SM, SM, VM, HBM, VM], out_specs=(HBM, VM, VM),
        scratch_shapes=[pltpu.VMEM((3, 2, 3, HALF, HALF), BF), pltpu.VMEM((PIX, HALF), F32),
                        pltpu.SemaphoreType.DMA((4, 2))],
        name="front_peer", compiler_params=params(14), cost_estimate=cost(5),
    )(core, eq, band, *in_hbm(weight), vec)


def attn_kernel(core_ref, eq_ref, act_own, act_peer, own_ref, peer_ref, x_ref, xp_ref, g_own, g_peer,
                wq_o, wq_p, wk_o, wk_p, wv_o, wv_p, wp_o, wp_p, vec_ref, out_own, out_peer, gmid_hbm,
                gconv_ref, small_ref, dquery, dkey, dvalue, mixed, normed_ref, weight, gfull, query,
                keys, values, gmixed, probs, gscores, gnormed, mid_ref, taps, band, x_own, x_peer,
                stat_ref, sems):
    core = core_ref[0]
    groups = [tap_copies(core, own_ref, peer_ref, taps, sems.at[5:8], down) for down in range(3)]
    start_all(groups[0])
    extra = [fetch(x_ref.at[core], x_own, sems.at[4, 2]), fetch(xp_ref.at[core], x_peer, sems.at[4, 3])]
    fill_bands(band, lambda row: both_rows(act_own, act_peer, row), eq_ref)
    start_all(groups[1])
    start_all(groups[2])
    wait_all(extra)
    for down in range(3):
        wait_all(groups[down])
        if down == 0:
            copies = []
            for index, (own, peer) in enumerate(
                    ((wq_o, wq_p), (wk_o, wk_p), (wv_o, wv_p), (wp_o, wp_p))):
                copies += start_all(
                    weight_copies(core, own, peer, weight.at[index], sems.at[index], ()))
            copies.append(fetch(g_own.at[core], gfull.at[:, 0:HALF], sems.at[4, 0]))
            copies.append(fetch(g_peer.at[core], gfull.at[:, HALF:C], sems.at[4, 1]))

        def conv(half, carry, down=down):
            at = half_rows(half)
            value = dot(tap_band(band, half, down),
                        taps[3 * down : 3 * down + 3].reshape(3 * C, C))
            if down > 0:
                value = value + mid_ref[at, :]
            else:
                value = value + vec_ref[5:6, :] + jnp.concatenate(
                    [x_own[at, :], x_peer[at, :]], 1).astype(F32)
            mid_ref[at, :] = value
            return carry

        lax.fori_loop(0, 2, conv, 0)
    norm_forward(lambda row: mid_ref[at_row(row), :], (normed_ref,), stat_ref, eq_ref,
                 vec_ref[6:7, :], vec_ref[7:8, :], lambda v: v)
    wait_all(copies)
    normed = normed_ref[...]
    query[...] = (dot(normed, weight[0]) + vec_ref[8:9, :]).astype(BF)
    keys[...] = dot(normed, weight[1]).astype(BF)
    values[...] = (dot(normed, weight[2]) + vec_ref[9:10, :]).astype(BF)
    gmixed[...] = dot_nt(gfull[...], weight[3]).astype(BF)

    rows = 256
    spot = lax.broadcasted_iota(jnp.int32, (1, PIX), 1)
    right = (spot & (SIDE - 1)) >= 16
    low = spot >= PIX // 2

    def block(index, carry):
        start = pl.multiple_of(index * rows, rows)
        at = pl.ds(start, rows)
        half = (start >= PIX // 2).astype(jnp.int32) * 2
        bias = []
        for side in range(2):
            base = (half + side) * 4
            row = jnp.where(low, jnp.where(right, eq_ref[base + 3], eq_ref[base + 2]),
                            jnp.where(right, eq_ref[base + 1], eq_ref[base]))
            bias.append(jnp.where(row > 0.5, 0.0, -1e30).reshape(1, 1, 1, PIX))
        bias = jnp.concatenate(bias, 1)
        scores = dot_nt(query[at, :], keys[...]) * (SCALE * LOG2E)
        scores = (scores.reshape(rows // SIDE, 2, 16, PIX) + bias).reshape(rows, PIX)
        expo = jnp.exp2(scores - jnp.max(scores, axis=1, keepdims=True))
        wide = expo * (1.0 / jnp.sum(expo, axis=1, keepdims=True))
        narrow = wide.astype(BF)
        probs[at, :] = narrow
        mixed[at, :] = dot(narrow, values[...]).astype(BF)
        gprobs = dot_nt(gmixed[at, :], values[...])
        delta = jnp.sum(wide * gprobs, axis=1, keepdims=True)
        grads = (wide * (gprobs - delta)).astype(BF)
        gscores[at, :] = grads
        dquery[at, :] = (dot(grads, keys[...]) * SCALE).astype(BF)
        return carry

    lax.fori_loop(0, PIX // rows, block, 0)

    def total(value):
        return jnp.sum(value.astype(F32), axis=0, keepdims=True)

    dkey[...] = (dot_tn(gscores[...], query[...]) * SCALE).astype(BF)
    dvalue[...] = dot_tn(probs[...], gmixed[...]).astype(BF)
    gnormed[...] = (dot_nt(dquery[...], weight[0]) + dot_nt(dkey[...], weight[1])
                    + dot_nt(dvalue[...], weight[2]))
    dbq, dbv, dbp = total(dquery[...]), total(dvalue[...]), total(gfull[...])

    out = mid_ref[...] + dot(mixed[...], weight[3]) + vec_ref[10:11, :]
    out_own[...] = out[:, :HALF]
    out_peer[...] = out[:, HALF:]

    def finish(row, change):
        grad = gfull[at_row(row), :].astype(F32) + change
        gnormed[at_row(row), :] = grad
        gconv_ref[at_row(row), :] = grad.astype(BF)

    dgain, dshift = norm_backward(
        lambda row: mid_ref[at_row(row), :], lambda row: gnormed[at_row(row), :], None, stat_ref,
        eq_ref, vec_ref[6:7, :], vec_ref[7:8, :], False, finish)
    store = fetch(gnormed, gmid_hbm, sems.at[4, 3])
    small_ref[...] = jnp.concatenate(
        [dgain, dshift, dbq, dbv, dbp, total(gconv_ref[...]), dbq, dbq], 0)
    store.wait()


def attn_call(core, eq, acts, own, peer, x, g, weights, vec):
    flat = [w for pair_of in weights for w in pair_of]
    return pl.pallas_call(
        attn_kernel,
        out_shape=(shape(PIX, HALF, F32), shape(PIX, HALF, F32), pltpu.HBM((PIX, C), F32),
                   shape(PIX, C, BF), shape(8, C, F32)) + (pltpu.VMEM((PIX, C), BF),) * 5,
        in_specs=[SM, SM, VM, VM] + [HBM] * 14 + [VM],
        out_specs=(VM, VM, HBM) + (VM,) * 7,
        scratch_shapes=[pltpu.VMEM((4, C, C), BF)] + [pltpu.VMEM((PIX, C), BF)] * 5
        + [pltpu.VMEM((PIX, PIX), BF)] * 2 + [pltpu.VMEM((PIX, C), F32)] * 2
        + [pltpu.VMEM((9, C, C), BF), pltpu.VMEM((2, BAND, 3 * C), BF)]
        + [pltpu.VMEM((PIX, HALF), BF)] * 2
        + [pltpu.VMEM((8, C), F32), pltpu.SemaphoreType.DMA((8, 4))],
        name="attention", compiler_params=params(34), cost_estimate=cost(28),
    )(core, eq, *acts, *in_hbm(own, peer, *x, *g, *flat), vec)


def attn_wgrad_kernel(core_ref, normed_ref, dquery, dkey, dvalue, mixed, g_own, g_peer, dw_own,
                      dw_peer, g_mine, g_back, sems):
    core = core_ref[0]
    copies = [fetch(g_own.at[core], g_mine, sems.at[0]), fetch(g_peer.at[core], g_back, sems.at[1])]
    normed = normed_ref[...]
    for index, ref in enumerate((dquery, dkey, dvalue)):
        full = dot_tn(normed, ref[...]).astype(BF)
        for local in range(2):
            target = pl.multiple_of(index * C + (core ^ local) * HALF, HALF)
            part = full[local * HALF : (local + 1) * HALF, :]
            dw_own[pl.ds(target, HALF), :] = part[:, :HALF]
            dw_peer[pl.ds(target, HALF), :] = part[:, HALF:]
    for copy in copies:
        copy.wait()
    for local, ref in enumerate((g_mine, g_back)):
        target = pl.multiple_of(3 * C + (core ^ local) * HALF, HALF)
        part = dot_tn(mixed[...], ref[...]).astype(BF)
        dw_own[pl.ds(target, HALF), :] = part[:HALF]
        dw_peer[pl.ds(target, HALF), :] = part[HALF:]


def attn_wgrad_call(core, normed, dquery, dkey, dvalue, mixed, g):
    return pl.pallas_call(
        attn_wgrad_kernel, out_shape=(shape(4 * C, HALF, BF),) * 2,
        in_specs=[SM] + [VM] * 5 + [HBM] * 2, out_specs=(VM, VM),
        scratch_shapes=[pltpu.VMEM((PIX, HALF), BF)] * 2 + [pltpu.SemaphoreType.DMA((2,))],
        name="attention_weights", compiler_params=params(6), cost_estimate=cost(3),
    )(core, normed, dquery, dkey, dvalue, mixed, *in_hbm(*g))


def fetch_all(sources, targets, sems):
    return [fetch(source, target, sems.at[index])
            for index, (source, target) in enumerate(zip(sources, targets))]


def wgrad2_kernel(core_ref, eq_ref, *refs):
    sources, (out_ref, act_mine, act_other, grad_mine, grad_other, band, band_other, sems) = (
        refs[:4], refs[4:])
    core = core_ref[0]
    copies = fetch_all(sources, (act_mine, act_other, grad_mine, grad_other), sems)
    copies[0].wait()
    fill_bands(band, lambda row: act_mine[at_row(row), :], eq_ref.at[0])
    copies[1].wait()
    fill_bands(band_other, lambda row: act_other[at_row(row), :], eq_ref.at[1])
    for copy in copies[2:]:
        copy.wait()

    def body(down, carry):
        for local in range(2):
            full = 0.0
            for half in range(2):
                rows = slice(half * (PIX // 2), (half + 1) * (PIX // 2))
                full = full + dot_tn(tap_band(band, half, down),
                                     grad_mine[rows, local * HALF : (local + 1) * HALF])
                full = full + dot_tn(tap_band(band_other, half, down),
                                     grad_other[rows, (1 - local) * HALF : (2 - local) * HALF])
            full = full.astype(BF)
            for index in range(3):
                base = (3 * down + index) * C + (core ^ local) * HALF
                out_ref[pl.ds(pl.multiple_of(base, HALF), HALF), :] = full[
                    index * HALF : (index + 1) * HALF]
        return carry

    lax.fori_loop(0, 3, body, 0)


def wgrad2_call(core, eqs, *arrays):
    return pl.pallas_call(
        wgrad2_kernel, out_shape=shape(9 * C, HALF, BF), in_specs=[SM, SM] + [HBM] * 4,
        out_specs=VM,
        scratch_shapes=[pltpu.VMEM((PIX, HALF), BF)] * 2 + [pltpu.VMEM((PIX, C), BF)] * 2
        + [pltpu.VMEM((2, BAND, 3 * HALF), BF)] * 2 + [pltpu.SemaphoreType.DMA((4,))],
        name="wgrad2", compiler_params=params(14), cost_estimate=cost(7),
    )(core, eqs, *in_hbm(*arrays))


TAPS = 6


def wgrad1_kernel(core_ref, eq_ref, *refs):
    sources, (out_ref, tail_ref, band, band_other, act, act2, grad_mine, grad_other, sems) = (
        refs[:6], refs[6:])
    core = core_ref[0]
    copies = fetch_all(sources, (grad_mine, grad_other, act.at[:, 0:HALF], act.at[:, HALF:C],
                                 act2.at[:, 0:HALF], act2.at[:, HALF:C]), sems)
    copies[0].wait()
    fill_bands(band, lambda row: grad_mine[at_row(row), :], eq_ref.at[0])
    copies[1].wait()
    fill_bands(band_other, lambda row: grad_other[at_row(row), :], eq_ref.at[1])
    for copy in copies[2:]:
        copy.wait()

    def group(down, out, base):
        full = 0.0
        for half in range(2):
            rows = slice(half * (PIX // 2), (half + 1) * (PIX // 2))
            full = full + dot_tn(act[rows, :], tap_band(band, half, down))
            full = full + dot_tn(act2[rows, :], tap_band(band_other, half, down))
        full = full.astype(BF)
        for index in range(3):
            for local in range(2):
                where = base + (2 - index) * C + (core ^ local) * HALF
                out[pl.ds(pl.multiple_of(where, HALF), HALF), :] = full[
                    local * HALF : (local + 1) * HALF, index * HALF : (index + 1) * HALF]

    group(0, tail_ref, 0)

    def body(down, carry):
        group(down, out_ref, (2 - down) * 3 * C)
        return carry

    lax.fori_loop(1, 3, body, 0)


def wgrad1_call(core, eqs, *arrays):
    return pl.pallas_call(
        wgrad1_kernel, out_shape=(shape(TAPS * C, HALF, BF), shape((9 - TAPS) * C, HALF, BF)),
        in_specs=[SM, SM] + [HBM] * 6, out_specs=(VM, VM),
        scratch_shapes=[pltpu.VMEM((2, BAND, 3 * HALF), BF)] * 2 + [pltpu.VMEM((PIX, C), BF)] * 2
        + [pltpu.VMEM((PIX, HALF), BF)] * 2 + [pltpu.SemaphoreType.DMA((6,))],
        name="wgrad1", compiler_params=params(16), cost_estimate=cost(7),
    )(core, eqs, *in_hbm(*arrays))


def dgrad_kernel(first, core_ref, eq_ref, own_ref, peer_ref, vec_ref, *refs):
    if first:
        (grad_own, grad_peer, stat_own, stat_peer, x_hbm, xp_hbm, gmid_hbm, out_own, out_peer, small_ref, weight, patch,
         total, stat_ref, sems, x_own, x_peer, gmid_ref) = refs
        load = lambda row: both_rows(x_own, x_peer, row)
        load_grad = lambda row: both_rows(grad_own, grad_peer, row)
        sources = (x_hbm.at[core_ref[0]], xp_hbm.at[core_ref[0]], gmid_hbm)
        held = (x_own, x_peer, gmid_ref)
        gain, shift = vec_ref[0:1, :], vec_ref[1:2, :]
    else:
        (grad_ref, stat_own, stat_peer, in_own, in_peer, out_own, out_peer, small_ref, weight, patch,
         total, stat_ref, sems, mine, back) = refs
        load = lambda row: both_rows(mine, back, row)
        load_grad = lambda row: grad_ref[at_row(row), :]
        sources, held = (in_own, in_peer), (mine, back)
        gain, shift = vec_ref[3:4, :], vec_ref[4:5, :]
    stat_ref[:, :HALF] = stat_own[...]
    stat_ref[:, HALF:] = stat_peer[...]
    copies = [tap_copies(core_ref[0], own_ref, peer_ref, weight, sems, 2 - down)
              for down in range(3)]
    for group in copies:
        for copy in group:
            copy.start()
    later = fetch_all(sources, held, sems.at[3])
    fill_bands(patch, load_grad, eq_ref)
    for down in range(3):
        for copy in copies[down]:
            copy.wait()

        def body(half, carry, down=down):
            value = total[half_rows(half), :] if down > 0 else 0.0
            for t in range(3):
                value = value + dot_nt(tap_band(patch, half, down)[:, t * C : (t + 1) * C],
                                       weight[8 - (3 * down + t)])
            total[half_rows(half), :] = value
            return carry

        lax.fori_loop(0, 2, body, 0)
    for copy in later:
        copy.wait()

    def finish(row, change):
        at = at_row(row)
        if first:
            change = change + gmid_ref[at, :]
        out_own[at, :] = change[:, :HALF].astype(out_own.dtype)
        out_peer[at, :] = change[:, HALF:].astype(out_peer.dtype)

    dgain, dshift = norm_backward(load, lambda row: total[at_row(row), :], total, stat_ref, eq_ref,
                                  gain, shift, True, finish)
    bias = [jnp.sum(ref[...].astype(F32), axis=0, keepdims=True) for ref in (out_own, out_peer)]
    bias = jnp.concatenate(bias, 1)
    small_ref[...] = jnp.concatenate([dgain, dshift, bias] + [dgain] * 5, 0)


def dgrad_call(core, eq, grad, own, peer, vec, stats, source, gmid=None):
    first = gmid is not None
    extra = (*source, gmid) if first else source
    held = [pltpu.VMEM((PIX, HALF), BF if first else F32)] * 2
    held += [pltpu.VMEM((PIX, C), F32)] if first else []
    outs = (shape(PIX, HALF, F32 if first else BF),) * 2
    return pl.pallas_call(
        functools.partial(dgrad_kernel, first),
        out_shape=outs + (shape(8, C, F32),),
        in_specs=[SM, SM, HBM, HBM, VM] + [VM] * (len(grad) + len(stats)) + [HBM] * len(extra),
        out_specs=(VM,) * 3,
        scratch_shapes=[pltpu.VMEM((9, C, C), BF), pltpu.VMEM((2, BAND, 3 * C), BF),
                        pltpu.VMEM((PIX, C), F32), pltpu.VMEM((8, C), F32),
                        pltpu.SemaphoreType.DMA((4, 4))] + held,
        name="dgrad1" if first else "dgrad2", compiler_params=params(16), cost_estimate=cost(10),
    )(core, eq, *in_hbm(own, peer), vec, *grad, *stats, *in_hbm(*extra))


EVERY, TIED, SMALL_FROM = "asrf", 9, 0
ORDERS = {
    "second": ((2, 0, 1), (0, 1, 2)),
    "attn": ((1, 2, 0), (1, 2, 0)),
    "first": ((2, 0, 1), (0, 1, 2)),
    "rest": ((1, 2, 0), (1, 2, 0)),
}


def orders_of(kind, size):
    bits = size.bit_length() - 1
    return [[*order, *range(3, bits)] for order in ORDERS[kind]]


def exchange(array, orders, stage, size):
    moves = [((d, c), (d ^ (1 << orders[c][stage]), c)) for d in range(size) for c in range(2)]
    return lax.ppermute(array, ("dp", "chan"), [(a[0] * 2 + a[1], b[0] * 2 + b[1]) for a, b in moves])


def side_of(orders, stage):
    bit = jnp.where(lax.axis_index("chan") == 0, orders[0][stage], orders[1][stage])
    return (lax.axis_index("dp") >> bit) & 1


def side_base(orders):
    base = 0
    for stage in range(len(orders[0])):
        base = base * 2 + side_of(orders, stage)
    return base


class Chain:
    def __init__(self, part, kind, size):
        self.value, self.size, self.orders, self.step = part, size, orders_of(kind, size), 0
        self.stages, self.rows = len(self.orders[0]), part.shape[0]

    def advance(self):
        stage = self.step if self.step < self.stages else 2 * self.stages - 1 - self.step
        if self.step < self.stages:
            half = self.value.shape[0] // 2
            side = side_of(self.orders, stage)
            send = lax.dynamic_slice_in_dim(self.value, (1 - side) * half, half, 0)
            keep = lax.dynamic_slice_in_dim(self.value, side * half, half, 0)
            self.value = keep + exchange(send, self.orders, stage, self.size)
        else:
            back = exchange(self.value, self.orders, stage, self.size)
            self.value = jnp.concatenate([self.value, back], 0) if stage > 0 else (self.value, back)
        self.step += 1


def together(chains, *values):
    held = lax.optimization_barrier(([c.value for c in chains], values))
    for chain, value in zip(chains, held[0]):
        chain.value = value
    return held[1]


def after(value, *others):
    return lax.optimization_barrier((value, *others))[0]


def spread_kernel(plan, base_ref, *refs):
    count = len(plan)
    ins, out_hbm, wide, sems = refs[:count], refs[-2 * count - 1], refs[-2 * count : -count], refs[-count:]
    copies = []
    for index, (start, first, rows) in enumerate(plan):
        wide[index][...] = ins[index][...].astype(F32)
        for block in range(ins[index].shape[0] // rows):
            row = start + ((block + first) ^ base_ref[index]) * rows
            copies.append(fetch(
                wide[index].at[block * rows : (block + 1) * rows, :],
                out_hbm.at[pl.ds(pl.multiple_of(row, rows & -rows), rows), :],
                sems[index].at[block]))
    wait_all(copies)


def spread(parts, rows, token, into=None):
    plan = [(start, first, chain.rows // chain.size) for _, chain, start, first in parts]
    arrays = [part[0] for part in parts]
    base = jnp.stack([side_base(part[1].orders) for part in parts]).astype(jnp.int32)
    held = () if into is None else (into,)
    return pl.pallas_call(
        functools.partial(spread_kernel, plan), out_shape=pltpu.HBM((rows, HALF), F32),
        in_specs=[SM] + [VM] * len(arrays) + [HBM] * len(held), out_specs=HBM,
        input_output_aliases={} if into is None else {1 + len(arrays): 0},
        scratch_shapes=[pltpu.VMEM(array.shape, F32) for array in arrays]
        + [pltpu.SemaphoreType.DMA((array.shape[0] // one[2],)) for array, one in zip(arrays, plan)],
        compiler_params=params(14), name="spread", cost_estimate=cost(2),
    )(after(base, token), *arrays, *held)


def second_target(row):
    return 0, row // C * HALF + row % HALF, slice(row // HALF % 2 * HALF, (row // HALF % 2 + 1) * HALF)


def attn_target(row):
    if row < 3 * C:
        return row // C, row % C, slice(0, HALF)
    row -= 3 * C
    return 3, row % HALF, slice(row // HALF * HALF, (row // HALF + 1) * HALF)


def place_kernel(size, targets, base_ref, *refs):
    ins, outs, held = refs[: 2 * len(targets)], refs[2 * len(targets) : -1], refs[-1]
    start = 0
    for index, target in enumerate(targets):
        part, part2 = ins[2 * index : 2 * index + 2]
        half = part.shape[0]
        held[start : start + half, :] = part[...]
        held[start + half : start + 2 * half, :] = part2[...]
        rows = 2 * half // size
        piece = math.gcd(rows, HALF)
        for row in range(0, 2 * half, piece):
            source = ((row // rows) ^ base_ref[index]) * rows + row % rows + start
            which, at, columns = target(row)
            outs[which][at : at + piece, columns] = held[
                pl.ds(pl.multiple_of(source, piece), piece), :].astype(F32)
        start += 2 * half


def place(chains, targets, shapes, token):
    parts = [part for chain in chains for part in chain.value]
    rows = sum(part.shape[0] for part in parts)
    base = jnp.stack([side_base(chain.orders) for chain in chains]).astype(jnp.int32)
    return pl.pallas_call(
        functools.partial(place_kernel, chains[0].size, targets),
        out_shape=tuple(shape(*one, F32) for one in shapes), in_specs=[SM] + [VM] * len(parts),
        out_specs=(VM,) * len(shapes), scratch_shapes=[pltpu.VMEM((rows, HALF), BF)],
        compiler_params=params(12), name="place", cost_estimate=cost(2),
    )(after(base, token), *parts)


def swap(array):
    return lax.ppermute(array, "chan", [(0, 1), (1, 0)])


def shards(pixels, tile_ids, first_gain, first_shift, first_conv, first_bias, second_gain,
           second_shift, second_conv, second_bias, attn_gain, attn_shift, query_weight,
           query_bias, key_weight, value_weight, value_bias, proj_weight, proj_bias, cotangent,
           *, size):
    index = lax.axis_index("chan")
    core = index.reshape(1).astype(jnp.int32)
    tiles = tile_ids.reshape(2, 2, 16, 2, 16)[:, :, 0, :, 0].reshape(2, 4)
    eqs = (tiles[:, :, None] == tiles[:, None, :]).astype(F32).reshape(2, 16)
    eqs = jnp.where(index == 0, eqs, eqs[::-1])
    own_vectors = jnp.stack([first_gain, first_shift, first_bias, second_gain, second_shift,
                             second_bias, attn_gain, attn_shift, query_bias, value_bias, proj_bias])
    pixels_peer = swap(pixels)
    pixels_peer, own_vectors, eqs = lax.optimization_barrier((pixels_peer, own_vectors, eqs))
    eq = eqs[0]
    peer_vectors = swap(own_vectors)
    first_conv, peer_vectors, pixels_peer = lax.optimization_barrier(
        (first_conv, peer_vectors, pixels_peer))
    first_peer = swap(first_conv)
    weights = lax.optimization_barrier(
        (query_weight, key_weight, value_weight, proj_weight, peer_vectors))[:4]
    weights_peer = [swap(array) for array in weights]
    vectors = jnp.concatenate([own_vectors, peer_vectors], 1)
    x = (pixels, pixels_peer)
    act_own, act_peer, stat_own, stat_peer, band, conv1_own, act2_own, stat2_own = front_call(
        core, eq, *x, first_conv, own_vectors, peer_vectors)
    first_peer, act2_own, act_own, act_peer, second_conv, cotangent, *weights_peer = (
        lax.optimization_barrier((first_peer, act2_own, act_own, act_peer, second_conv, cotangent,
                                  *weights_peer)))
    second_peer, g_peer = swap(second_conv), swap(cotangent)
    act_other = (swap(act_peer), swap(act_own))
    conv1_peer, act2_peer, stat2_peer = front_peer_call(core, eq, band, first_peer, peer_vectors)
    act2_peer, second_peer, g_peer = lax.optimization_barrier((act2_peer, second_peer, g_peer))
    g = (cotangent, g_peer)
    act2_other = swap(act2_peer)
    out_own, out_peer, gmid, gconv2, small3, *parts, normed = attn_call(
        core, eq, (act2_own, act2_peer), second_conv, second_peer, x, g,
        list(zip(weights, weights_peer)), vectors)
    gconv2, act2_other, *act_other = lax.optimization_barrier((gconv2, act2_other, *act_other))
    gconv2_other = swap(gconv2)
    dattn, dattn_peer = attn_wgrad_call(core, normed, *parts, g)
    dattn, gconv2, gconv2_other = lax.optimization_barrier((dattn, gconv2, gconv2_other))
    attn_other = swap(dattn_peer)
    part = wgrad2_call(core, eqs, act2_own, act2_other, gconv2, gconv2_other)
    attn_other, part = lax.optimization_barrier((attn_other, part))
    second, attn_sum = Chain(part, "second", size), Chain(dattn + attn_other, "attn", size)
    (gconv2,) = together([second, attn_sum], gconv2)

    for chain in (attn_sum, second):
        chain.advance()
    gconv1_own, gconv1_peer, small2 = dgrad_call(
        core, eq, (gconv2,), second_conv, second_peer, vectors, (stat2_own, stat2_peer),
        (conv1_own, conv1_peer))
    gconv1_other = swap(gconv1_peer)
    gconv1_own, gconv1_other = together([second, attn_sum], gconv1_own, gconv1_other)

    for chain in (attn_sum, second):
        chain.advance()
    part, tail = wgrad1_call(core, eqs, gconv1_own, gconv1_other, act_own, act_peer, *act_other)
    first, rest = Chain(part, "first", size), Chain(tail, "rest", size)
    (gconv1_own,) = together([second, attn_sum, first, rest], gconv1_own)

    known = {"a": attn_sum, "s": second, "r": rest, "f": first}
    every = [known[name] for name in EVERY]
    for chain in every:
        chain.advance()
    pix_own, pix_peer, small1 = dgrad_call(core, eq, (gconv1_own, gconv1_peer), first_conv,
                                           first_peer, vectors, (stat_own, stat_peer), x, gmid)
    small = jnp.concatenate([small1, small2, small3], 0)
    pix_peer, out_peer, small = together(every, pix_peer, out_peer, small)

    small = small[:, :HALF] + swap(small[:, HALF:])
    pix_back = swap(pix_peer)
    out_back = swap(out_peer)
    bits = size.bit_length() - 1
    turn, bit = 0, 0
    token = core
    while any(chain.step < 2 * bits for chain in every):
        for chain in every:
            if chain.step < 2 * bits:
                chain.advance()
                if turn < TIED:
                    (token,) = together([chain], token)
        if turn >= SMALL_FROM and bit < bits:
            small = small + lax.ppermute(
                small, "dp", [(i, i ^ (1 << bit)) for i in range(size)])
            small, token = lax.optimization_barrier((small, token))
            bit += 1
        turn += 1
    (sums2,) = place([second], [second_target], [(9 * HALF, C)], core)
    sums3 = place([attn_sum], [attn_target], [(C, HALF), (C, HALF), (C, HALF), (HALF, C)], core)
    mine, back = first.value
    half = size // 2
    sums1 = spread([(rest.value[0], rest, TAPS * C, 0), (rest.value[1], rest, TAPS * C, half),
                    (mine, first, 0, 0)], 9 * C, core)
    back, sums1, sums2, *sums3 = lax.optimization_barrier((back, sums1, sums2, *sums3))
    sums1 = spread([(back, first, 0, half)], 9 * C, token, sums1)

    def unboth(own, back):
        return jnp.where(index == 0, jnp.stack([own, back]), jnp.stack([back, own]))

    return (
        unboth(out_own, out_back), unboth(pix_own, pix_back), small[0], small[1],
        sums1.reshape(9, C, HALF), small[10], small[8], small[9], sums2.reshape(9, HALF, C),
        small[21], small[16], small[17], sums3[0], small[18], sums3[1], sums3[2], small[19],
        sums3[3], small[20],
    )


def solution(mesh):
    chan = P("chan")
    rows = P("dp", None, "chan")
    return jax.shard_map(
        functools.partial(shards, size=mesh.shape["dp"]),
        mesh=mesh,
        in_specs=(
            rows, P("dp", None), chan, chan, P(None, None, "chan"), chan, chan, chan,
            P(None, "chan", None), chan, chan, chan, P(None, "chan"), chan, P(None, "chan"),
            P(None, "chan"), chan, P("chan", None), chan, rows,
        ),
        out_specs=(
            rows, rows, chan, chan, P(None, None, "chan"), chan, chan, chan,
            P(None, "chan", None), chan, chan, chan, P(None, "chan"), chan, P(None, "chan"),
            P(None, "chan"), chan, P("chan", None), chan,
        ),
        check_vma=False,
    )
```

profile of v0, /device:TPU:0, one launch (start us, length us, event | category | flops | bytes accessed | tf_op | source)
XLA Modules:
  0.0 215.1 jit_solution(5110416036379097997)
XLA Ops:
  6.5 10.3 %front.1 = (bf16[1024,256]{1,0:T(8,128)(2,1)}, bf16[1024,256]{1,0:T(8,128)(2,1)}, f32[8,256]{1,0:T(8,128)S(1)}, f32[8,256]{1,0:T(8,128)S(1)}, bf16[2,576,1536]{2...) custom-call(s32[1]{0:T(128)} %bitcast.core_ref, ...), custom_call_target="tpu_custom_call" | custom-call | flops 9900000256 | bytes 1048576 | tf_op jit(solution)/shard_map/front/pallas_call | solution.py:351
  18.4 6.5 %front_peer.1 = (f32[1024,256]{1,0:T(8,128)}, bf16[1024,256]{1,0:T(8,128)(2,1)S(1)}, f32[8,256]{1,0:T(8,128)S(1)}) custom-call(s32[1]{0:T(128)} %bitcast.core_ref, f32[16]{0:T(128)S(1)} %slice_bitcast_fusion.eq_ref, bf16[2,576,1536]{2,1,0:T(8,128)(2,1)S(1)} %get-tuple-element.166.band, bf16[9,512,256]{2,1,0:T(8,128)(2,1)} %copy-done.4, ...), custom_call_target="tpu_custom_call" | custom-call | flops 5500000256 | bytes 1048576 | tf_op jit(solution)/shard_map/front_peer/pallas_call | solution.py:366
  26.7 28.4 %attention.1 = (f32[1024,256]{1,0:T(8,128)S(1)}, f32[1024,256]{1,0:T(8,128)S(1)}, f32[1024,512]{1,0:T(8,128)}, bf16[1024,512]{1,0:T(8,128)(2,1)}, f32[8,512]{1,0...) custom-call(s32[1]{0:T(128)} %bitcast.core_ref, ...), custom_call_target="tpu_custom_call" | custom-call | flops 30799998976 | bytes 1048576 | tf_op jit(solution)/shard_map/attention/pallas_call | solution.py:483
  55.6 4.3 %attention_weights.1 = (bf16[2048,256]{1,0:T(8,128)(2,1)S(1)}, bf16[2048,256]{1,0:T(8,128)(2,1)}) custom-call(s32[1]{0:T(128)} %bitcast.core_ref, bf16[1024,512]{1,0:T(8,128)(2,1)S(1)} %get-tuple-element.179.normed_ref, bf16[1024,512]{1,0:T(8,128)(2,1)S(1)} %get-tuple-element.180.dquery, bf16[1024,512]{1,0:T(8,128)(2,1)S(1)} %get-tuple-element.181.dkey, ...), custom_call_target="tpu_custom_call" | custom-call | flops 3300000000 | bytes 1048576 | tf_op jit(solution)/shard_map/attention_weights/pallas_call | solution.py:520
  60.1 8.0 %wgrad2.1 = bf16[4608,256]{1,0:T(8,128)(2,1)S(1)} custom-call(s32[1]{0:T(128)} %bitcast.core_ref, f32[2,16]{1,0:T(2,128)S(1)} %broadcast_select_fusion.eq_ref, bf16[1024,256]{1,0:T(8,128)(2,1)} %copy-done, bf16[1024,256]{1,0:T(8,128)(2,1)} %copy-done.11, bf16[1024,512]{1,0:T(8,128)(2,1)} %get-tuple-element.198.refs_2_.refs_0_, ...), custom_call_target="tpu_custom_call" | custom-call | flops 7699999744 | bytes 1048576 | tf_op jit(solution)/shard_map/wgrad2/pallas_call | solution.py:565
  69.8 3.0 %collective-permute-start.14 = (bf16[2304,256]{1,0:T(8,128)(2,1)S(1)}, bf16[2304,256]{1,0:T(8,128)(2,1)S(1)}, u32[]{:S(2)}, u32[]{:S(2)}) collective-permute-start(bf16[2304,256]{1,0:T(8,128)(2,1)S(1)} %constant_dynamic-slice_fusion.15), channel_id=1, source_target_pairs={{0,8},{1,3},{2,10},{3,1},{4,12},{5,7},{6,14},{7,5},{8,0},{9,11},{1... | collective-permute-start | bytes 3538952 | tf_op jit(solution)/shard_map/ppermute | solution.py:711
  74.4 11.5 %dgrad2.1 = (bf16[1024,256]{1,0:T(8,128)(2,1)S(1)}, bf16[1024,256]{1,0:T(8,128)(2,1)S(1)}, f32[8,512]{1,0:T(8,128)S(1)}) custom-call(s32[1]{0:T(128)} %bitcast.core_ref, f32[16]{0:T(128)S(1)} %slice_bitcast_fusion.eq_ref, bf16[9,256,512]{2,1,0:T(8,128)(2,1)} %own_ref.1, bf16[9,256,512]{2,1,0:T(8,128)(2,1)} %copy-done.5, ...), custom_call_target="tpu_custom_call" | custom-call | flops 11000000512 | bytes 1048576 | tf_op jit(solution)/shard_map/dgrad2/pallas_call | solution.py:683
  91.0 8.2 %wgrad1.1 = (bf16[3072,256]{1,0:T(8,128)(2,1)S(1)}, bf16[1536,256]{1,0:T(8,128)(2,1)S(1)}) custom-call(s32[1]{0:T(128)} %bitcast.core_ref, f32[2,16]{1,0:T(2,128)S(1)} %broadcast_select_fusion.eq_ref, bf16[1024,256]{1,0:T(8,128)(2,1)} %copy-done.1, bf16[1024,256]{1,0:T(8,128)(2,1)} %copy-done.12, bf16[1024,256]{1,0:T(8,128)(2,1)} %get-tuple-element.187.refs_2_, ...), custom_call_target="tpu_custom_call" | custom-call | flops 7699999744 | bytes 1048576 | tf_op jit(solution)/shard_map/wgrad1/pallas_call | solution.py:613
  103.8 10.9 %dgrad1.1 = (f32[1024,256]{1,0:T(8,128)S(1)}, f32[1024,256]{1,0:T(8,128)S(1)}, f32[8,512]{1,0:T(8,128)S(1)}) custom-call(s32[1]{0:T(128)} %bitcast.core_ref, f32[16]{0:T(128)S(1)} %slice_bitcast_fusion.eq_ref, bf16[9,512,256]{2,1,0:T(8,128)(2,1)} %own_ref.2, bf16[9,512,256]{2,1,0:T(8,128)(2,1)} %copy-done.4, ...), custom_call_target="tpu_custom_call" | custom-call | flops 11000000512 | bytes 1048576 | tf_op jit(solution)/shard_map/dgrad1/pallas_call | solution.py:683
  117.0 2.6 %collective-permute-start.30 = (bf16[128,256]{1,0:T(8,128)(2,1)S(1)}, bf16[128,256]{1,0:T(8,128)(2,1)S(1)}, u32[]{:S(2)}, u32[]{:S(2)}) collective-permute-start(bf16[128,256]{1,0:T(8,128)(2,1)S(1)} %constant_dynamic-slice_fusion.4), channel_id=1, source_target_pairs={{0,16},{1,17},{2,18},{3,19},{4,20},{5,21},{6,22},{7,23},{8,24},{9,... | collective-permute-start | bytes 196616 | tf_op jit(solution)/shard_map/ppermute | solution.py:711
  120.7 3.1 %collective-permute-done.26 = f32[24,256]{1,0:T(8,128)S(1)} collective-permute-done((f32[24,256]{1,0:T(8,128)S(1)}, f32[24,256]{1,0:T(8,128)S(1)}, u32[]{:S(2)}, u32[]{:S(2)}) %collective-permute-start.26) | collective-permute-done | bytes 24608 | tf_op jit(solution)/shard_map/ppermute | solution.py:914
  125.3 2.7 %collective-permute-start.35 = (bf16[128,256]{1,0:T(8,128)(2,1)S(1)}, bf16[128,256]{1,0:T(8,128)(2,1)S(1)}, u32[]{:S(2)}, u32[]{:S(2)}) collective-permute-start(bf16[128,256]{1,0:T(8,128)(2,1)S(1)} %dynamic-slice_add_fusion.14), channel_id=1, source_target_pairs={{0,16},{1,17},{2,18},{3,19},{4,20},{5,21},{6,22},{7,23},{8,24},{9,... | collective-permute-start | bytes 196616 | tf_op jit(solution)/shard_map/ppermute | solution.py:711
  127.9 3.6 %collective-permute-start.36 = (f32[24,256]{1,0:T(8,128)S(1)}, f32[24,256]{1,0:T(8,128)S(1)}, u32[]{:S(2)}, u32[]{:S(2)}) collective-permute-start(f32[24,256]{1,0:T(8,128)S(1)} %add.231), channel_id=1, source_target_pairs={{0,8},{2,10},{4,12},{6,14},{8,0},{10,2},{12,4},{14,6},{16,24},{18,... | collective-permute-start | bytes 73736 | tf_op jit(solution)/shard_map/ppermute | solution.py:914
  137.4 2.7 %collective-permute-start.33 = (bf16[192,256]{1,0:T(8,128)(2,1)S(1)}, bf16[192,256]{1,0:T(8,128)(2,1)S(1)}, u32[]{:S(2)}, u32[]{:S(2)}) collective-permute-start(bf16[192,256]{1,0:T(8,128)(2,1)S(1)} %constant_dynamic-slice_fusion.2), channel_id=1, source_target_pairs={{0,2},{1,3},{2,0},{3,1},{4,6},{5,7},{6,4},{7,5},{8,10},{9,11},{10,... | collective-permute-start | bytes 294920 | tf_op jit(solution)/shard_map/ppermute | solution.py:711
  147.0 2.5 %collective-permute-done.38 = bf16[96,256]{1,0:T(8,128)(2,1)S(1)} collective-permute-done((bf16[96,256]{1,0:T(8,128)(2,1)S(1)}, bf16[96,256]{1,0:T(8,128)(2,1)S(1)}, u32[]{:S(2)}, u32[]{:S(2)}) %collective-permute-start.38) | collective-permute-done | bytes 49184 | tf_op jit(solution)/shard_map/ppermute | solution.py:711
  149.5 3.4 %collective-permute-start.46 = (bf16[96,256]{1,0:T(8,128)(2,1)S(1)}, bf16[96,256]{1,0:T(8,128)(2,1)S(1)}, u32[]{:S(2)}, u32[]{:S(2)}) collective-permute-start(bf16[96,256]{1,0:T(8,128)(2,1)S(1)} %dynamic-slice_add_fusion.15), channel_id=1, source_target_pairs={{0,16},{1,17},{2,18},{3,19},{4,20},{5,21},{6,22},{7,23},{8,24},{9,... | collective-permute-start | bytes 147464 | tf_op jit(solution)/shard_map/ppermute | solution.py:711
  157.0 4.5 %collective-permute-done.37 = bf16[192,256]{1,0:T(8,128)(2,1)S(1)} collective-permute-done((bf16[192,256]{1,0:T(8,128)(2,1)S(1)}, bf16[192,256]{1,0:T(8,128)(2,1)S(1)}, u32[]{:S(2)}, u32[]{:S(2)}) %collective-permute-start.37) | collective-permute-done | bytes 98336 | tf_op jit(solution)/shard_map/ppermute | solution.py:711
  163.3 6.3 %collective-permute-done.42 = bf16[192,256]{1,0:T(8,128)(2,1)S(1)} collective-permute-done((bf16[192,256]{1,0:T(8,128)(2,1)S(1)}, bf16[192,256]{1,0:T(8,128)(2,1)S(1)}, u32[]{:S(2)}, u32[]{:S(2)}) %collective-permute-start.42) | collective-permute-done | bytes 98336 | tf_op jit(solution)/shard_map/ppermute | solution.py:711
  171.2 4.1 %collective-permute-done.43 = bf16[384,256]{1,0:T(8,128)(2,1)S(1)} collective-permute-done((bf16[384,256]{1,0:T(8,128)(2,1)S(1)}, bf16[384,256]{1,0:T(8,128)(2,1)S(1)}, u32[]{:S(2)}, u32[]{:S(2)}) %collective-permute-start.43) | collective-permute-done | bytes 196640 | tf_op jit(solution)/shard_map/ppermute | solution.py:711
  178.1 5.8 %collective-permute-done.44 = bf16[768,256]{1,0:T(8,128)(2,1)S(1)} collective-permute-done((bf16[768,256]{1,0:T(8,128)(2,1)S(1)}, bf16[768,256]{1,0:T(8,128)(2,1)S(1)}, u32[]{:S(2)}, u32[]{:S(2)}) %collective-permute-start.44) | collective-permute-done | bytes 393248 | tf_op jit(solution)/shard_map/ppermute | solution.py:711
  193.4 7.0 %collective-permute-done.49.refs_1_ = bf16[768,256]{1,0:T(8,128)(2,1)S(1)} collective-permute-done((bf16[768,256]{1,0:T(8,128)(2,1)S(1)}, bf16[768,256]{1,0:T(8,128)(2,1)S(1)}, u32[]{:S(2)}, u32[]{:S(2)}) %collective-permute-start.49) | collective-permute-done | bytes 393248 | tf_op jit(solution)/shard_map/ppermute | solution.py:711
  200.4 8.0 %collective-permute-done.45.refs_0_ = bf16[1536,256]{1,0:T(8,128)(2,1)S(1)} collective-permute-done((bf16[1536,256]{1,0:T(8,128)(2,1)S(1)}, bf16[1536,256]{1,0:T(8,128)(2,1)S(1)}, u32[]{:S(2)}, u32[]{:S(2)}) %collective-permute-start.45) | collective-permute-done | bytes 786464 | tf_op jit(solution)/shard_map/ppermute | solution.py:711
  208.5 2.4 %spread.2.refs_1_ = f32[4608,256]{1,0:T(8,128)} custom-call(s32[3]{0:T(128)S(1)} %pad_add_fusion.base_ref, bf16[768,256]{1,0:T(8,128)(2,1)S(1)} %pad_maximum_fusion.5.refs_0_, bf16[768,256]{1,0:T(8,128)(2,1)S(1)} %collective-permute-done.49.refs_1_, bf16[1536,256]{1,0:T(8,128)(2,1)S(1)} %pad_maximum_fusion.1.refs_2_), custom_call_target="tpu_custom_call" | custom-call | flops 2200000000 | bytes 1048576 | tf_op jit(solution)/shard_map/spread/pallas_call | solution.py:776
  210.9 2.7 %place.2 = f32[2304,512]{1,0:T(8,128)} custom-call(s32[1]{0:T(128)} %bitcast.19.base_ref, bf16[2304,256]{1,0:T(8,128)(2,1)S(1)} %pad_maximum_fusion.refs_0_, bf16[2304,256]{1,0:T(8,128)(2,1)S(1)} %collective-permute-done.51.refs_1_), custom_call_target="tpu_custom_call" | custom-call | flops 2200000000 | bytes 1048576 | tf_op jit(solution)/shard_map/place/pallas_call | solution.py:819
  (197 shorter events, 60.9 us)
Async XLA Ops:
  5.3 11.6 %collective-permute-start.2 = (bf16[9,512,256]{2,1,0:T(8,128)(2,1)}, bf16[9,512,256]{2,1,0:T(8,128)(2,1)S(1)}, u32[]{:S(2)}, u32[]{:S(2)}) collective-permute-start(bf16[9,512,256]{2,1,0:T(8,128)(2,1)} %own_ref.2), channel_id=1, source_target_pairs={{0,1},{1,0},{2,3},{3,2},{4,5},{5,4},{6,7},{7,6},{8,9},{9,8},{10,11... | collective-permute-start | bytes 7077896 | tf_op jit(solution)/shard_map/ppermute | solution.py:828
  5.4 11.4 %collective-permute-start.3 = (bf16[512,256]{1,0:T(8,128)(2,1)}, bf16[512,256]{1,0:T(8,128)(2,1)S(1)}, u32[]{:S(2)}, u32[]{:S(2)}) collective-permute-start(bf16[512,256]{1,0:T(8,128)(2,1)} %wq_o), channel_id=1, source_target_pairs={{0,1},{1,0},{2,3},{3,2},{4,5},{5,4},{6,7},{7,6},{8,9},{9,8},{10,11... | collective-permute-start | bytes 786440 | tf_op jit(solution)/shard_map/ppermute | solution.py:828
  17.5 37.6 %collective-permute-start.11 = (bf16[1024,256]{1,0:T(8,128)(2,1)}, bf16[1024,256]{1,0:T(8,128)(2,1)S(1)}, u32[]{:S(2)}, u32[]{:S(2)}) collective-permute-start(bf16[1024,256]{1,0:T(8,128)(2,1)} %get-tuple-element.186.refs_3_), channel_id=1, source_target_pairs={{0,1},{1,0},{2,3},{3,2},{4,5},{5,4},{6,7},{7,6},{8,9},{9,8},{10,11... | collective-permute-start | bytes 1572872 | tf_op jit(solution)/shard_map/ppermute | solution.py:828
  17.8 37.3 %collective-permute-start.12 = (bf16[1024,256]{1,0:T(8,128)(2,1)}, bf16[1024,256]{1,0:T(8,128)(2,1)S(1)}, u32[]{:S(2)}, u32[]{:S(2)}) collective-permute-start(bf16[1024,256]{1,0:T(8,128)(2,1)} %get-tuple-element.187.refs_2_), channel_id=1, source_target_pairs={{0,1},{1,0},{2,3},{3,2},{4,5},{5,4},{6,7},{7,6},{8,9},{9,8},{10,11... | collective-permute-start | bytes 1572872 | tf_op jit(solution)/shard_map/ppermute | solution.py:828
  25.0 30.1 %collective-permute-start.10 = (bf16[1024,256]{1,0:T(8,128)(2,1)S(1)}, bf16[1024,256]{1,0:T(8,128)(2,1)S(1)}, u32[]{:S(2)}, u32[]{:S(2)}) collective-permute-start(bf16[1024,256]{1,0:T(8,128)(2,1)S(1)} %get-tuple-element.171.act_peer), channel_id=1, source_target_pairs={{0,1},{1,0},{2,3},{3,2},{4,5},{5,4},{6,7},{7,6},{8,9},{9,8},{10,11... | collective-permute-start | bytes 1572872 | tf_op jit(solution)/shard_map/ppermute | solution.py:828
  69.8 17.2 %collective-permute-start.14 = (bf16[2304,256]{1,0:T(8,128)(2,1)S(1)}, bf16[2304,256]{1,0:T(8,128)(2,1)S(1)}, u32[]{:S(2)}, u32[]{:S(2)}) collective-permute-start(bf16[2304,256]{1,0:T(8,128)(2,1)S(1)} %constant_dynamic-slice_fusion.15), channel_id=1, source_target_pairs={{0,8},{1,3},{2,10},{3,1},{4,12},{5,7},{6,14},{7,5},{8,0},{9,11},{1... | collective-permute-start | bytes 3538952 | tf_op jit(solution)/shard_map/ppermute | solution.py:711
  72.8 13.9 %collective-permute-start.15 = (bf16[1024,256]{1,0:T(8,128)(2,1)S(1)}, bf16[1024,256]{1,0:T(8,128)(2,1)S(1)}, u32[]{:S(2)}, u32[]{:S(2)}) collective-permute-start(bf16[1024,256]{1,0:T(8,128)(2,1)S(1)} %constant_dynamic-slice_fusion.14), channel_id=1, source_target_pairs={{0,4},{1,5},{2,6},{3,7},{4,0},{5,1},{6,2},{7,3},{8,12},{9,13},{10,... | collective-permute-start | bytes 1572872 | tf_op jit(solution)/shard_map/ppermute | solution.py:711
  99.6 15.2 %collective-permute-start.19 = (bf16[256,256]{1,0:T(8,128)(2,1)S(1)}, bf16[256,256]{1,0:T(8,128)(2,1)S(1)}, u32[]{:S(2)}, u32[]{:S(2)}) collective-permute-start(bf16[256,256]{1,0:T(8,128)(2,1)S(1)} %constant_dynamic-slice_fusion.11), channel_id=1, source_target_pairs={{0,2},{1,3},{2,0},{3,1},{4,6},{5,7},{6,4},{7,5},{8,10},{9,11},{10,... | collective-permute-start | bytes 393224 | tf_op jit(solution)/shard_map/ppermute | solution.py:711
  100.4 14.4 %collective-permute-start.20 = (bf16[576,256]{1,0:T(8,128)(2,1)S(1)}, bf16[576,256]{1,0:T(8,128)(2,1)S(1)}, u32[]{:S(2)}, u32[]{:S(2)}) collective-permute-start(bf16[576,256]{1,0:T(8,128)(2,1)S(1)} %constant_dynamic-slice_fusion.10), channel_id=1, source_target_pairs={{0,4},{1,9},{2,6},{3,11},{4,0},{5,13},{6,2},{7,15},{8,12},{9,1},{1... | collective-permute-start | bytes 884744 | tf_op jit(solution)/shard_map/ppermute | solution.py:711
  101.8 13.1 %collective-permute-start.21 = (bf16[768,256]{1,0:T(8,128)(2,1)S(1)}, bf16[768,256]{1,0:T(8,128)(2,1)S(1)}, u32[]{:S(2)}, u32[]{:S(2)}) collective-permute-start(bf16[768,256]{1,0:T(8,128)(2,1)S(1)} %constant_dynamic-slice_fusion.9), channel_id=1, source_target_pairs={{0,4},{1,5},{2,6},{3,7},{4,0},{5,1},{6,2},{7,3},{8,12},{9,13},{10,... | collective-permute-start | bytes 1179656 | tf_op jit(solution)/shard_map/ppermute | solution.py:711
  102.6 12.4 %collective-permute-start.22 = (bf16[1536,256]{1,0:T(8,128)(2,1)S(1)}, bf16[1536,256]{1,0:T(8,128)(2,1)S(1)}, u32[]{:S(2)}, u32[]{:S(2)}) collective-permute-start(bf16[1536,256]{1,0:T(8,128)(2,1)S(1)} %constant_dynamic-slice_fusion.8), channel_id=1, source_target_pairs={{0,8},{1,3},{2,10},{3,1},{4,12},{5,7},{6,14},{7,5},{8,0},{9,11},{1... | collective-permute-start | bytes 2359304 | tf_op jit(solution)/shard_map/ppermute | solution.py:711
  115.4 29.8 %collective-permute-start.27 = (bf16[768,256]{1,0:T(8,128)(2,1)S(1)}, bf16[768,256]{1,0:T(8,128)(2,1)S(1)}, u32[]{:S(2)}, u32[]{:S(2)}) collective-permute-start(bf16[768,256]{1,0:T(8,128)(2,1)S(1)} %constant_dynamic-slice_fusion.7), channel_id=1, source_target_pairs={{0,2},{1,5},{2,0},{3,7},{4,6},{5,1},{6,4},{7,3},{8,10},{9,13},{10,... | collective-permute-start | bytes 1179656 | tf_op jit(solution)/shard_map/ppermute | solution.py:711
  120.2 15.6 %collective-permute-start.29 = (bf16[288,256]{1,0:T(8,128)(2,1)S(1)}, bf16[288,256]{1,0:T(8,128)(2,1)S(1)}, u32[]{:S(2)}, u32[]{:S(2)}) collective-permute-start(bf16[288,256]{1,0:T(8,128)(2,1)S(1)} %constant_dynamic-slice_fusion.5), channel_id=1, source_target_pairs={{0,16},{1,17},{2,18},{3,19},{4,20},{5,21},{6,22},{7,23},{8,24},{9,... | collective-permute-start | bytes 442376 | tf_op jit(solution)/shard_map/ppermute | solution.py:711
  134.0 36.7 %collective-permute-start.41 = (f32[24,256]{1,0:T(8,128)S(1)}, f32[24,256]{1,0:T(8,128)S(1)}, u32[]{:S(2)}, u32[]{:S(2)}) collective-permute-start(f32[24,256]{1,0:T(8,128)S(1)} %add.238), channel_id=1, source_target_pairs={{0,16},{2,18},{4,20},{6,22},{8,24},{10,26},{12,28},{14,30},{16,0},... | collective-permute-start | bytes 73736 | tf_op jit(solution)/shard_map/ppermute | solution.py:914
  140.2 35.8 %collective-permute-start.52 = (bf16[512,256]{1,0:T(8,128)(2,1)S(1)}, bf16[512,256]{1,0:T(8,128)(2,1)S(1)}, u32[]{:S(2)}, u32[]{:S(2)}) collective-permute-start(bf16[512,256]{1,0:T(8,128)(2,1)S(1)} %pad_maximum_fusion.7), channel_id=1, source_target_pairs={{0,8},{1,9},{2,10},{3,11},{4,12},{5,13},{6,14},{7,15},{8,0},{9,1},... | collective-permute-start | bytes 786440 | tf_op jit(solution)/shard_map/ppermute | solution.py:711
  144.7 16.9 %collective-permute-start.39 = (bf16[576,256]{1,0:T(8,128)(2,1)S(1)}, bf16[576,256]{1,0:T(8,128)(2,1)S(1)}, u32[]{:S(2)}, u32[]{:S(2)}) collective-permute-start(bf16[576,256]{1,0:T(8,128)(2,1)S(1)} %pad_maximum_fusion.6), channel_id=1, source_target_pairs={{0,4},{1,9},{2,6},{3,11},{4,0},{5,13},{6,2},{7,15},{8,12},{9,1},{1... | collective-permute-start | bytes 884744 | tf_op jit(solution)/shard_map/ppermute | solution.py:711
  155.2 15.5 %collective-permute-start.47 = (bf16[192,256]{1,0:T(8,128)(2,1)S(1)}, bf16[192,256]{1,0:T(8,128)(2,1)S(1)}, u32[]{:S(2)}, u32[]{:S(2)}) collective-permute-start(bf16[192,256]{1,0:T(8,128)(2,1)S(1)} %pad_maximum_fusion.11), channel_id=1, source_target_pairs={{0,2},{1,3},{2,0},{3,1},{4,6},{5,7},{6,4},{7,5},{8,10},{9,11},{10,... | collective-permute-start | bytes 294920 | tf_op jit(solution)/shard_map/ppermute | solution.py:711
  161.6 15.5 %collective-permute-start.50 = (bf16[1152,256]{1,0:T(8,128)(2,1)S(1)}, bf16[1152,256]{1,0:T(8,128)(2,1)S(1)}, u32[]{:S(2)}, u32[]{:S(2)}) collective-permute-start(bf16[1152,256]{1,0:T(8,128)(2,1)S(1)} %pad_maximum_fusion.2), channel_id=1, source_target_pairs={{0,2},{1,5},{2,0},{3,7},{4,6},{5,1},{6,4},{7,3},{8,10},{9,13},{10,... | collective-permute-start | bytes 1769480 | tf_op jit(solution)/shard_map/ppermute | solution.py:711
  170.6 16.0 %collective-permute-start.23 = (f32[1024,256]{1,0:T(8,128)S(1)}, f32[1024,256]{1,0:T(8,128)S(1)}, u32[]{:S(2)}, u32[]{:S(2)}) collective-permute-start(f32[1024,256]{1,0:T(8,128)S(1)} %get-tuple-element.226), channel_id=1, source_target_pairs={{0,1},{1,0},{2,3},{3,2},{4,5},{5,4},{6,7},{7,6},{8,9},{9,8},{10,11... | collective-permute-start | bytes 3145736 | tf_op jit(solution)/shard_map/ppermute | solution.py:828
  170.7 18.6 %collective-permute-start.24 = (f32[1024,256]{1,0:T(8,128)S(1)}, f32[1024,256]{1,0:T(8,128)S(1)}, u32[]{:S(2)}, u32[]{:S(2)}) collective-permute-start(f32[1024,256]{1,0:T(8,128)S(1)} %get-tuple-element.228), channel_id=1, source_target_pairs={{0,1},{1,0},{2,3},{3,2},{4,5},{5,4},{6,7},{7,6},{8,9},{9,8},{10,11... | collective-permute-start | bytes 3145736 | tf_op jit(solution)/shard_map/ppermute | solution.py:828
  177.1 14.9 %collective-permute-start.53 = (bf16[1024,256]{1,0:T(8,128)(2,1)S(1)}, bf16[1024,256]{1,0:T(8,128)(2,1)S(1)}, u32[]{:S(2)}, u32[]{:S(2)}) collective-permute-start(bf16[1024,256]{1,0:T(8,128)(2,1)S(1)} %pad_maximum_fusion.3.refs_0_), channel_id=1, source_target_pairs={{0,4},{1,5},{2,6},{3,7},{4,0},{5,1},{6,2},{7,3},{8,12},{9,13},{10,... | collective-permute-start | bytes 1572872 | tf_op jit(solution)/shard_map/ppermute | solution.py:711
  183.9 27.1 %collective-permute-start.51 = (bf16[2304,256]{1,0:T(8,128)(2,1)S(1)}, bf16[2304,256]{1,0:T(8,128)(2,1)S(1)}, u32[]{:S(2)}, u32[]{:S(2)}) collective-permute-start(bf16[2304,256]{1,0:T(8,128)(2,1)S(1)} %pad_maximum_fusion.refs_0_), channel_id=1, source_target_pairs={{0,8},{1,3},{2,10},{3,1},{4,12},{5,7},{6,14},{7,5},{8,0},{9,11},{1... | collective-permute-start | bytes 3538952 | tf_op jit(solution)/shard_map/ppermute | solution.py:711
  185.4 23.1 %collective-permute-start.45 = (bf16[1536,256]{1,0:T(8,128)(2,1)S(1)}, bf16[1536,256]{1,0:T(8,128)(2,1)S(1)}, u32[]{:S(2)}, u32[]{:S(2)}) collective-permute-start(bf16[1536,256]{1,0:T(8,128)(2,1)S(1)} %pad_maximum_fusion.1.refs_2_), channel_id=1, source_target_pairs={{0,8},{1,3},{2,10},{3,1},{4,12},{5,7},{6,14},{7,5},{8,0},{9,11},{1... | collective-permute-start | bytes 2359304 | tf_op jit(solution)/shard_map/ppermute | solution.py:711
  186.7 13.8 %collective-permute-start.49 = (bf16[768,256]{1,0:T(8,128)(2,1)S(1)}, bf16[768,256]{1,0:T(8,128)(2,1)S(1)}, u32[]{:S(2)}, u32[]{:S(2)}) collective-permute-start(bf16[768,256]{1,0:T(8,128)(2,1)S(1)} %pad_maximum_fusion.5.refs_0_), channel_id=1, source_target_pairs={{0,4},{1,5},{2,6},{3,7},{4,0},{5,1},{6,2},{7,3},{8,12},{9,13},{10,... | collective-permute-start | bytes 1179656 | tf_op jit(solution)/shard_map/ppermute | solution.py:711
  (47 other events, 300.3 us)
where the time goes:
time: 215 us
  Pallas kernels  96 us (45%)
  starting transfers between devices  56 us (26%)
  waiting for transfers between devices  48.7 us (23%)
  other arithmetic  6.54 us (3%)
  local copies, waits for them, and re-layouts  6.34 us (3%)
    ppermute x32, starting transfers between devices, exchange(): lax.ppermute(array, ('dp', 'chan'), [(a[0] * 2 + a[1], b[0] * 2 + b[1]) f...  45.6 us
    ppermute x32, waiting for transfers between devices, exchange(): lax.ppermute(array, ('dp', 'chan'), [(a[0] * 2 + a[1], b[0] * 2 + b[1]) f...  40.8 us
    pallas_call x1, Pallas kernels, attn_call(): pl.pallas_call(attn_kernel, out_shape=(shape(PIX, HALF, F32), shape(PIX,...  28.4 us
    pallas_call x2, Pallas kernels, dgrad_call(): pl.pallas_call(functools.partial(dgrad_kernel, first), out_shape=outs + (...  22.4 us
    pallas_call x1, Pallas kernels, front_call(): pl.pallas_call(front_kernel, out_shape=(half, half, shape(8, HALF, F32),...  10.3 us
    pallas_call x1, Pallas kernels, wgrad1_call(): pl.pallas_call(wgrad1_kernel, out_shape=(shape(TAPS * C, HALF, BF), shape...  8.24 us
    pallas_call x1, Pallas kernels, wgrad2_call(): pl.pallas_call(wgrad2_kernel, out_shape=shape(9 * C, HALF, BF), in_specs=...  8.01 us
    pallas_call x1, Pallas kernels, front_peer_call(): pl.pallas_call(front_peer_kernel, out_shape=(pltpu.HBM((PIX, HALF), F32),...  6.51 us
  transfers between devices with their start and end apart: 54, of which 17 were waited for; matrix products, arithmetic and copies ran while one was open for 4% of the time, Pallas kernels for 43%

commit v1 on v0

--- a/solution.py
+++ b/solution.py
@@ -419,7 +419,7 @@
     values[...] = (dot(normed, weight[2]) + vec_ref[9:10, :]).astype(BF)
     gmixed[...] = dot_nt(gfull[...], weight[3]).astype(BF)
 
-    rows = 256
+    rows = 512
     spot = lax.broadcasted_iota(jnp.int32, (1, PIX), 1)
     right = (spot & (SIDE - 1)) >= 16
     low = spot >= PIX // 2
@@ -491,7 +491,7 @@
         + [pltpu.VMEM((9, C, C), BF), pltpu.VMEM((2, BAND, 3 * C), BF)]
         + [pltpu.VMEM((PIX, HALF), BF)] * 2
         + [pltpu.VMEM((8, C), F32), pltpu.SemaphoreType.DMA((8, 4))],
-        name="attention", compiler_params=params(34), cost_estimate=cost(28),
+        name="attention", compiler_params=params(40), cost_estimate=cost(28),
     )(core, eq, *acts, *in_hbm(own, peer, *x, *g, *flat), vec)
 
 
@@ -920,10 +920,8 @@
     sums3 = place([attn_sum], [attn_target], [(C, HALF), (C, HALF), (C, HALF), (HALF, C)], core)
     mine, back = first.value
     half = size // 2
-    sums1 = spread([(rest.value[0], rest, TAPS * C, 0), (rest.value[1], rest, TAPS * C, half),
-                    (mine, first, 0, 0)], 9 * C, core)
-    back, sums1, sums2, *sums3 = lax.optimization_barrier((back, sums1, sums2, *sums3))
-    sums1 = spread([(back, first, 0, half)], 9 * C, token, sums1)
+    sums1 = spread([(rest.value[0], rest, TAPS * C, 0), (mine, first, 0, 0)], 9 * C, core)
+    sums1 = spread([(rest.value[1], rest, TAPS * C, half), (back, first, 0, half)], 9 * C, token, sums1)
 
     def unboth(own, back):
         return jnp.where(index == 0, jnp.stack([own, back]), jnp.stack([back, own]))

time: 215 us -> 215 us (level)
  starting transfers between devices: 56 us -> 51.8 us
  waiting for transfers between devices: 48.7 us -> 52.6 us
    ppermute x32, waiting for transfers between devices: 40.8 us -> 47.8 us  [exchange(): lax.ppermute(array, ('dp', 'chan'), [(a[0] * 2 + a[1], b[0] * 2 + b[1]) f...]
    ppermute x4, waiting for transfers between devices: 5.33 us -> 2.28 us  [shards(): lax.ppermute(small, 'dp', [(i, i ^ 1 << bit) for i in range(size)])]
    ppermute x32, starting transfers between devices: 45.6 us -> 43.1 us  [exchange(): lax.ppermute(array, ('dp', 'chan'), [(a[0] * 2 + a[1], b[0] * 2 + b[1]) f...]
where the time goes in v1:
time: 215 us
  Pallas kernels  95.5 us (44%)
  waiting for transfers between devices  52.6 us (24%)
  starting transfers between devices  51.8 us (24%)
  local copies, waits for them, and re-layouts  6.77 us (3%)
  other arithmetic  6.53 us (3%)
    ppermute x32, waiting for transfers between devices, exchange(): lax.ppermute(array, ('dp', 'chan'), [(a[0] * 2 + a[1], b[0] * 2 + b[1]) f...  47.8 us
    ppermute x32, starting transfers between devices, exchange(): lax.ppermute(array, ('dp', 'chan'), [(a[0] * 2 + a[1], b[0] * 2 + b[1]) f...  43.1 us
    pallas_call x1, Pallas kernels, attn_call(): pl.pallas_call(attn_kernel, out_shape=(shape(PIX, HALF, F32), shape(PIX,...  27.2 us
    pallas_call x2, Pallas kernels, dgrad_call(): pl.pallas_call(functools.partial(dgrad_kernel, first), out_shape=outs + (...  22.7 us
    pallas_call x1, Pallas kernels, front_call(): pl.pallas_call(front_kernel, out_shape=(half, half, shape(8, HALF, F32),...  10.3 us
    pallas_call x1, Pallas kernels, wgrad1_call(): pl.pallas_call(wgrad1_kernel, out_shape=(shape(TAPS * C, HALF, BF), shape...  8.24 us
    pallas_call x1, Pallas kernels, wgrad2_call(): pl.pallas_call(wgrad2_kernel, out_shape=shape(9 * C, HALF, BF), in_specs=...  8.01 us
    pallas_call x1, Pallas kernels, front_peer_call(): pl.pallas_call(front_peer_kernel, out_shape=(pltpu.HBM((PIX, HALF), F32),...  6.51 us
  transfers between devices with their start and end apart: 54, of which 17 were waited for; matrix products, arithmetic and copies ran while one was open for 4% of the time, Pallas kernels for 43%

profile of v1, /device:TPU:0, one launch (start us, length us, event | category | flops | bytes accessed | tf_op | source)
XLA Modules:
  0.0 214.6 jit_solution(11975779382642968274)
XLA Ops:
  6.5 10.3 %front.1 = (bf16[1024,256]{1,0:T(8,128)(2,1)}, bf16[1024,256]{1,0:T(8,128)(2,1)}, f32[8,256]{1,0:T(8,128)S(1)}, f32[8,256]{1,0:T(8,128)S(1)}, bf16[2,576,1536]{2...) custom-call(s32[1]{0:T(128)} %bitcast.core_ref, ...), custom_call_target="tpu_custom_call" | custom-call | flops 9900000256 | bytes 1048576 | tf_op jit(solution)/shard_map/front/pallas_call | solution.py:351
  18.4 6.5 %front_peer.1 = (f32[1024,256]{1,0:T(8,128)}, bf16[1024,256]{1,0:T(8,128)(2,1)S(1)}, f32[8,256]{1,0:T(8,128)S(1)}) custom-call(s32[1]{0:T(128)} %bitcast.core_ref, f32[16]{0:T(128)S(1)} %slice_bitcast_fusion.eq_ref, bf16[2,576,1536]{2,1,0:T(8,128)(2,1)S(1)} %get-tuple-element.159.band, bf16[9,512,256]{2,1,0:T(8,128)(2,1)} %copy-done.4, ...), custom_call_target="tpu_custom_call" | custom-call | flops 5500000256 | bytes 1048576 | tf_op jit(solution)/shard_map/front_peer/pallas_call | solution.py:366
  26.7 27.2 %attention.1 = (f32[1024,256]{1,0:T(8,128)S(1)}, f32[1024,256]{1,0:T(8,128)S(1)}, f32[1024,512]{1,0:T(8,128)}, bf16[1024,512]{1,0:T(8,128)(2,1)}, f32[8,512]{1,0...) custom-call(s32[1]{0:T(128)} %bitcast.core_ref, ...), custom_call_target="tpu_custom_call" | custom-call | flops 30799998976 | bytes 1048576 | tf_op jit(solution)/shard_map/attention/pallas_call | solution.py:483
  54.8 4.3 %attention_weights.1 = (bf16[2048,256]{1,0:T(8,128)(2,1)S(1)}, bf16[2048,256]{1,0:T(8,128)(2,1)}) custom-call(s32[1]{0:T(128)} %bitcast.core_ref, bf16[1024,512]{1,0:T(8,128)(2,1)S(1)} %get-tuple-element.172.normed_ref, bf16[1024,512]{1,0:T(8,128)(2,1)S(1)} %get-tuple-element.173.dquery, bf16[1024,512]{1,0:T(8,128)(2,1)S(1)} %get-tuple-element.174.dkey, ...), custom_call_target="tpu_custom_call" | custom-call | flops 3300000000 | bytes 1048576 | tf_op jit(solution)/shard_map/attention_weights/pallas_call | solution.py:520
  59.5 8.0 %wgrad2.1 = bf16[4608,256]{1,0:T(8,128)(2,1)S(1)} custom-call(s32[1]{0:T(128)} %bitcast.core_ref, f32[2,16]{1,0:T(2,128)S(1)} %broadcast_select_fusion.eq_ref, bf16[1024,256]{1,0:T(8,128)(2,1)} %copy-done, bf16[1024,256]{1,0:T(8,128)(2,1)} %copy-done.11, bf16[1024,512]{1,0:T(8,128)(2,1)} %get-tuple-element.191.refs_2_.refs_0_, ...), custom_call_target="tpu_custom_call" | custom-call | flops 7699999744 | bytes 1048576 | tf_op jit(solution)/shard_map/wgrad2/pallas_call | solution.py:565
  69.2 2.8 %collective-permute-start.14 = (bf16[2304,256]{1,0:T(8,128)(2,1)S(1)}, bf16[2304,256]{1,0:T(8,128)(2,1)S(1)}, u32[]{:S(2)}, u32[]{:S(2)}) collective-permute-start(bf16[2304,256]{1,0:T(8,128)(2,1)S(1)} %constant_dynamic-slice_fusion.15), channel_id=1, source_target_pairs={{0,8},{1,3},{2,10},{3,1},{4,12},{5,7},{6,14},{7,5},{8,0},{9,11},{1... | collective-permute-start | bytes 3538952 | tf_op jit(solution)/shard_map/ppermute | solution.py:711
  73.6 11.5 %dgrad2.1 = (bf16[1024,256]{1,0:T(8,128)(2,1)S(1)}, bf16[1024,256]{1,0:T(8,128)(2,1)S(1)}, f32[8,512]{1,0:T(8,128)S(1)}) custom-call(s32[1]{0:T(128)} %bitcast.core_ref, f32[16]{0:T(128)S(1)} %slice_bitcast_fusion.eq_ref, bf16[9,256,512]{2,1,0:T(8,128)(2,1)} %own_ref.1, bf16[9,256,512]{2,1,0:T(8,128)(2,1)} %copy-done.5, ...), custom_call_target="tpu_custom_call" | custom-call | flops 11000000512 | bytes 1048576 | tf_op jit(solution)/shard_map/dgrad2/pallas_call | solution.py:683
  90.3 8.2 %wgrad1.1 = (bf16[3072,256]{1,0:T(8,128)(2,1)S(1)}, bf16[1536,256]{1,0:T(8,128)(2,1)S(1)}) custom-call(s32[1]{0:T(128)} %bitcast.core_ref, f32[2,16]{1,0:T(2,128)S(1)} %broadcast_select_fusion.eq_ref, bf16[1024,256]{1,0:T(8,128)(2,1)} %copy-done.1, bf16[1024,256]{1,0:T(8,128)(2,1)} %copy-done.12, bf16[1024,256]{1,0:T(8,128)(2,1)} %get-tuple-element.180.refs_2_, ...), custom_call_target="tpu_custom_call" | custom-call | flops 7699999744 | bytes 1048576 | tf_op jit(solution)/shard_map/wgrad1/pallas_call | solution.py:613
  103.1 11.2 %dgrad1.1 = (f32[1024,256]{1,0:T(8,128)S(1)}, f32[1024,256]{1,0:T(8,128)S(1)}, f32[8,512]{1,0:T(8,128)S(1)}) custom-call(s32[1]{0:T(128)} %bitcast.core_ref, f32[16]{0:T(128)S(1)} %slice_bitcast_fusion.eq_ref, bf16[9,512,256]{2,1,0:T(8,128)(2,1)} %own_ref.2, bf16[9,512,256]{2,1,0:T(8,128)(2,1)} %copy-done.4, ...), custom_call_target="tpu_custom_call" | custom-call | flops 11000000512 | bytes 1048576 | tf_op jit(solution)/shard_map/dgrad1/pallas_call | solution.py:683
  115.9 2.6 %collective-permute-start.30 = (bf16[128,256]{1,0:T(8,128)(2,1)S(1)}, bf16[128,256]{1,0:T(8,128)(2,1)S(1)}, u32[]{:S(2)}, u32[]{:S(2)}) collective-permute-start(bf16[128,256]{1,0:T(8,128)(2,1)S(1)} %constant_dynamic-slice_fusion.4), channel_id=1, source_target_pairs={{0,16},{1,17},{2,18},{3,19},{4,20},{5,21},{6,22},{7,23},{8,24},{9,... | collective-permute-start | bytes 196616 | tf_op jit(solution)/shard_map/ppermute | solution.py:711
  120.2 2.1 collective-permute-done.26
  123.7 2.4 %collective-permute-start.35 = (bf16[128,256]{1,0:T(8,128)(2,1)S(1)}, bf16[128,256]{1,0:T(8,128)(2,1)S(1)}, u32[]{:S(2)}, u32[]{:S(2)}) collective-permute-start(bf16[128,256]{1,0:T(8,128)(2,1)S(1)} %dynamic-slice_add_fusion.14), channel_id=1, source_target_pairs={{0,16},{1,17},{2,18},{3,19},{4,20},{5,21},{6,22},{7,23},{8,24},{9,... | collective-permute-start | bytes 196616 | tf_op jit(solution)/shard_map/ppermute | solution.py:711
  127.4 5.1 %collective-permute-start.27 = (bf16[768,256]{1,0:T(8,128)(2,1)S(1)}, bf16[768,256]{1,0:T(8,128)(2,1)S(1)}, u32[]{:S(2)}, u32[]{:S(2)}) collective-permute-start(bf16[768,256]{1,0:T(8,128)(2,1)S(1)} %constant_dynamic-slice_fusion.7), channel_id=1, source_target_pairs={{0,2},{1,5},{2,0},{3,7},{4,6},{5,1},{6,4},{7,3},{8,10},{9,13},{10,... | collective-permute-start | bytes 1179656 | tf_op jit(solution)/shard_map/ppermute | solution.py:711
  137.9 4.2 %collective-permute-done.40 = bf16[256,256]{1,0:T(8,128)(2,1)S(1)} collective-permute-done((bf16[256,256]{1,0:T(8,128)(2,1)S(1)}, bf16[256,256]{1,0:T(8,128)(2,1)S(1)}, u32[]{:S(2)}, u32[]{:S(2)}) %collective-permute-start.40) | collective-permute-done | bytes 131104 | tf_op jit(solution)/shard_map/ppermute | solution.py:711
  145.6 4.4 %collective-permute-done.38 = bf16[96,256]{1,0:T(8,128)(2,1)S(1)} collective-permute-done((bf16[96,256]{1,0:T(8,128)(2,1)S(1)}, bf16[96,256]{1,0:T(8,128)(2,1)S(1)}, u32[]{:S(2)}, u32[]{:S(2)}) %collective-permute-start.38) | collective-permute-done | bytes 49184 | tf_op jit(solution)/shard_map/ppermute | solution.py:711
  150.1 3.4 %collective-permute-start.42 = (bf16[96,256]{1,0:T(8,128)(2,1)S(1)}, bf16[96,256]{1,0:T(8,128)(2,1)S(1)}, u32[]{:S(2)}, u32[]{:S(2)}) collective-permute-start(bf16[96,256]{1,0:T(8,128)(2,1)S(1)} %dynamic-slice_add_fusion.15), channel_id=1, source_target_pairs={{0,16},{1,17},{2,18},{3,19},{4,20},{5,21},{6,22},{7,23},{8,24},{9,... | collective-permute-start | bytes 147464 | tf_op jit(solution)/shard_map/ppermute | solution.py:711
  157.7 3.9 %collective-permute-done.37 = bf16[192,256]{1,0:T(8,128)(2,1)S(1)} collective-permute-done((bf16[192,256]{1,0:T(8,128)(2,1)S(1)}, bf16[192,256]{1,0:T(8,128)(2,1)S(1)}, u32[]{:S(2)}, u32[]{:S(2)}) %collective-permute-start.37) | collective-permute-done | bytes 98336 | tf_op jit(solution)/shard_map/ppermute | solution.py:711
  162.7 6.1 %collective-permute-done.46 = bf16[192,256]{1,0:T(8,128)(2,1)S(1)} collective-permute-done((bf16[192,256]{1,0:T(8,128)(2,1)S(1)}, bf16[192,256]{1,0:T(8,128)(2,1)S(1)}, u32[]{:S(2)}, u32[]{:S(2)}) %collective-permute-start.46) | collective-permute-done | bytes 98336 | tf_op jit(solution)/shard_map/ppermute | solution.py:711
  170.3 4.2 %collective-permute-done.47 = bf16[384,256]{1,0:T(8,128)(2,1)S(1)} collective-permute-done((bf16[384,256]{1,0:T(8,128)(2,1)S(1)}, bf16[384,256]{1,0:T(8,128)(2,1)S(1)}, u32[]{:S(2)}, u32[]{:S(2)}) %collective-permute-start.47) | collective-permute-done | bytes 196640 | tf_op jit(solution)/shard_map/ppermute | solution.py:711
  177.6 5.4 %collective-permute-done.48 = bf16[768,256]{1,0:T(8,128)(2,1)S(1)} collective-permute-done((bf16[768,256]{1,0:T(8,128)(2,1)S(1)}, bf16[768,256]{1,0:T(8,128)(2,1)S(1)}, u32[]{:S(2)}, u32[]{:S(2)}) %collective-permute-start.48) | collective-permute-done | bytes 393248 | tf_op jit(solution)/shard_map/ppermute | solution.py:711
  189.6 2.4 %collective-permute-done.53.refs_1_ = bf16[1024,256]{1,0:T(8,128)(2,1)S(1)} collective-permute-done((bf16[1024,256]{1,0:T(8,128)(2,1)S(1)}, bf16[1024,256]{1,0:T(8,128)(2,1)S(1)}, u32[]{:S(2)}, u32[]{:S(2)}) %collective-permute-start.53) | collective-permute-done | bytes 524320 | tf_op jit(solution)/shard_map/ppermute | solution.py:711
  193.4 6.9 %collective-permute-done.45.refs_0_ = bf16[768,256]{1,0:T(8,128)(2,1)S(1)} collective-permute-done((bf16[768,256]{1,0:T(8,128)(2,1)S(1)}, bf16[768,256]{1,0:T(8,128)(2,1)S(1)}, u32[]{:S(2)}, u32[]{:S(2)}) %collective-permute-start.45) | collective-permute-done | bytes 393248 | tf_op jit(solution)/shard_map/ppermute | solution.py:711
  200.3 7.4 %collective-permute-done.49.refs_1_ = bf16[1536,256]{1,0:T(8,128)(2,1)S(1)} collective-permute-done((bf16[1536,256]{1,0:T(8,128)(2,1)S(1)}, bf16[1536,256]{1,0:T(8,128)(2,1)S(1)}, u32[]{:S(2)}, u32[]{:S(2)}) %collective-permute-start.49) | collective-permute-done | bytes 786464 | tf_op jit(solution)/shard_map/ppermute | solution.py:711
  211.9 2.7 %place.2 = f32[2304,512]{1,0:T(8,128)} custom-call(s32[1]{0:T(128)} %bitcast.20.base_ref, bf16[2304,256]{1,0:T(8,128)(2,1)S(1)} %pad_maximum_fusion.refs_0_, bf16[2304,256]{1,0:T(8,128)(2,1)S(1)} %collective-permute-done.51.refs_1_), custom_call_target="tpu_custom_call" | custom-call | flops 2200000000 | bytes 1048576 | tf_op jit(solution)/shard_map/place/pallas_call | solution.py:819
  (197 shorter events, 59.9 us)
Async XLA Ops:
  5.3 11.6 %collective-permute-start.2 = (bf16[9,512,256]{2,1,0:T(8,128)(2,1)}, bf16[9,512,256]{2,1,0:T(8,128)(2,1)S(1)}, u32[]{:S(2)}, u32[]{:S(2)}) collective-permute-start(bf16[9,512,256]{2,1,0:T(8,128)(2,1)} %own_ref.2), channel_id=1, source_target_pairs={{0,1},{1,0},{2,3},{3,2},{4,5},{5,4},{6,7},{7,6},{8,9},{9,8},{10,11... | collective-permute-start | bytes 7077896 | tf_op jit(solution)/shard_map/ppermute | solution.py:828
  17.5 36.4 %collective-permute-start.11 = (bf16[1024,256]{1,0:T(8,128)(2,1)}, bf16[1024,256]{1,0:T(8,128)(2,1)S(1)}, u32[]{:S(2)}, u32[]{:S(2)}) collective-permute-start(bf16[1024,256]{1,0:T(8,128)(2,1)} %get-tuple-element.179.refs_3_), channel_id=1, source_target_pairs={{0,1},{1,0},{2,3},{3,2},{4,5},{5,4},{6,7},{7,6},{8,9},{9,8},{10,11... | collective-permute-start | bytes 1572872 | tf_op jit(solution)/shard_map/ppermute | solution.py:828
  17.8 36.1 %collective-permute-start.12 = (bf16[1024,256]{1,0:T(8,128)(2,1)}, bf16[1024,256]{1,0:T(8,128)(2,1)S(1)}, u32[]{:S(2)}, u32[]{:S(2)}) collective-permute-start(bf16[1024,256]{1,0:T(8,128)(2,1)} %get-tuple-element.180.refs_2_), channel_id=1, source_target_pairs={{0,1},{1,0},{2,3},{3,2},{4,5},{5,4},{6,7},{7,6},{8,9},{9,8},{10,11... | collective-permute-start | bytes 1572872 | tf_op jit(solution)/shard_map/ppermute | solution.py:828
  25.0 28.9 %collective-permute-start.10 = (bf16[1024,256]{1,0:T(8,128)(2,1)S(1)}, bf16[1024,256]{1,0:T(8,128)(2,1)S(1)}, u32[]{:S(2)}, u32[]{:S(2)}) collective-permute-start(bf16[1024,256]{1,0:T(8,128)(2,1)S(1)} %get-tuple-element.164.act_peer), channel_id=1, source_target_pairs={{0,1},{1,0},{2,3},{3,2},{4,5},{5,4},{6,7},{7,6},{8,9},{9,8},{10,11... | collective-permute-start | bytes 1572872 | tf_op jit(solution)/shard_map/ppermute | solution.py:828
  69.2 17.0 %collective-permute-start.14 = (bf16[2304,256]{1,0:T(8,128)(2,1)S(1)}, bf16[2304,256]{1,0:T(8,128)(2,1)S(1)}, u32[]{:S(2)}, u32[]{:S(2)}) collective-permute-start(bf16[2304,256]{1,0:T(8,128)(2,1)S(1)} %constant_dynamic-slice_fusion.15), channel_id=1, source_target_pairs={{0,8},{1,3},{2,10},{3,1},{4,12},{5,7},{6,14},{7,5},{8,0},{9,11},{1... | collective-permute-start | bytes 3538952 | tf_op jit(solution)/shard_map/ppermute | solution.py:711
  72.1 13.9 %collective-permute-start.15 = (bf16[1024,256]{1,0:T(8,128)(2,1)S(1)}, bf16[1024,256]{1,0:T(8,128)(2,1)S(1)}, u32[]{:S(2)}, u32[]{:S(2)}) collective-permute-start(bf16[1024,256]{1,0:T(8,128)(2,1)S(1)} %constant_dynamic-slice_fusion.14), channel_id=1, source_target_pairs={{0,4},{1,5},{2,6},{3,7},{4,0},{5,1},{6,2},{7,3},{8,12},{9,13},{10,... | collective-permute-start | bytes 1572872 | tf_op jit(solution)/shard_map/ppermute | solution.py:711
  98.8 15.5 %collective-permute-start.19 = (bf16[256,256]{1,0:T(8,128)(2,1)S(1)}, bf16[256,256]{1,0:T(8,128)(2,1)S(1)}, u32[]{:S(2)}, u32[]{:S(2)}) collective-permute-start(bf16[256,256]{1,0:T(8,128)(2,1)S(1)} %constant_dynamic-slice_fusion.11), channel_id=1, source_target_pairs={{0,2},{1,3},{2,0},{3,1},{4,6},{5,7},{6,4},{7,5},{8,10},{9,11},{10,... | collective-permute-start | bytes 393224 | tf_op jit(solution)/shard_map/ppermute | solution.py:711
  99.6 14.7 %collective-permute-start.20 = (bf16[576,256]{1,0:T(8,128)(2,1)S(1)}, bf16[576,256]{1,0:T(8,128)(2,1)S(1)}, u32[]{:S(2)}, u32[]{:S(2)}) collective-permute-start(bf16[576,256]{1,0:T(8,128)(2,1)S(1)} %constant_dynamic-slice_fusion.10), channel_id=1, source_target_pairs={{0,4},{1,9},{2,6},{3,11},{4,0},{5,13},{6,2},{7,15},{8,12},{9,1},{1... | collective-permute-start | bytes 884744 | tf_op jit(solution)/shard_map/ppermute | solution.py:711
  101.0 13.4 %collective-permute-start.21 = (bf16[768,256]{1,0:T(8,128)(2,1)S(1)}, bf16[768,256]{1,0:T(8,128)(2,1)S(1)}, u32[]{:S(2)}, u32[]{:S(2)}) collective-permute-start(bf16[768,256]{1,0:T(8,128)(2,1)S(1)} %constant_dynamic-slice_fusion.9), channel_id=1, source_target_pairs={{0,4},{1,5},{2,6},{3,7},{4,0},{5,1},{6,2},{7,3},{8,12},{9,13},{10,... | collective-permute-start | bytes 1179656 | tf_op jit(solution)/shard_map/ppermute | solution.py:711
  101.9 12.7 %collective-permute-start.22 = (bf16[1536,256]{1,0:T(8,128)(2,1)S(1)}, bf16[1536,256]{1,0:T(8,128)(2,1)S(1)}, u32[]{:S(2)}, u32[]{:S(2)}) collective-permute-start(bf16[1536,256]{1,0:T(8,128)(2,1)S(1)} %constant_dynamic-slice_fusion.8), channel_id=1, source_target_pairs={{0,8},{1,3},{2,10},{3,1},{4,12},{5,7},{6,14},{7,5},{8,0},{9,11},{1... | collective-permute-start | bytes 2359304 | tf_op jit(solution)/shard_map/ppermute | solution.py:711
  114.9 22.4 %collective-permute-start.28 = (bf16[384,256]{1,0:T(8,128)(2,1)S(1)}, bf16[384,256]{1,0:T(8,128)(2,1)S(1)}, u32[]{:S(2)}, u32[]{:S(2)}) collective-permute-start(bf16[384,256]{1,0:T(8,128)(2,1)S(1)} %constant_dynamic-slice_fusion.6), channel_id=1, source_target_pairs={{0,8},{1,9},{2,10},{3,11},{4,12},{5,13},{6,14},{7,15},{8,0},{9,1},... | collective-permute-start | bytes 589832 | tf_op jit(solution)/shard_map/ppermute | solution.py:711
  119.8 15.3 %collective-permute-start.29 = (bf16[288,256]{1,0:T(8,128)(2,1)S(1)}, bf16[288,256]{1,0:T(8,128)(2,1)S(1)}, u32[]{:S(2)}, u32[]{:S(2)}) collective-permute-start(bf16[288,256]{1,0:T(8,128)(2,1)S(1)} %constant_dynamic-slice_fusion.5), channel_id=1, source_target_pairs={{0,16},{1,17},{2,18},{3,19},{4,20},{5,21},{6,22},{7,23},{8,24},{9,... | collective-permute-start | bytes 442376 | tf_op jit(solution)/shard_map/ppermute | solution.py:711
  127.4 16.9 %collective-permute-start.27 = (bf16[768,256]{1,0:T(8,128)(2,1)S(1)}, bf16[768,256]{1,0:T(8,128)(2,1)S(1)}, u32[]{:S(2)}, u32[]{:S(2)}) collective-permute-start(bf16[768,256]{1,0:T(8,128)(2,1)S(1)} %constant_dynamic-slice_fusion.7), channel_id=1, source_target_pairs={{0,2},{1,5},{2,0},{3,7},{4,6},{5,1},{6,4},{7,3},{8,10},{9,13},{10,... | collective-permute-start | bytes 1179656 | tf_op jit(solution)/shard_map/ppermute | solution.py:711
  132.5 37.2 %collective-permute-start.41 = (f32[24,256]{1,0:T(8,128)S(1)}, f32[24,256]{1,0:T(8,128)S(1)}, u32[]{:S(2)}, u32[]{:S(2)}) collective-permute-start(f32[24,256]{1,0:T(8,128)S(1)} %add.238), channel_id=1, source_target_pairs={{0,16},{2,18},{4,20},{6,22},{8,24},{10,26},{12,28},{14,30},{16,0},... | collective-permute-start | bytes 73736 | tf_op jit(solution)/shard_map/ppermute | solution.py:914
  142.1 33.1 %collective-permute-start.52 = (bf16[512,256]{1,0:T(8,128)(2,1)S(1)}, bf16[512,256]{1,0:T(8,128)(2,1)S(1)}, u32[]{:S(2)}, u32[]{:S(2)}) collective-permute-start(bf16[512,256]{1,0:T(8,128)(2,1)S(1)} %pad_maximum_fusion.7), channel_id=1, source_target_pairs={{0,8},{1,9},{2,10},{3,11},{4,12},{5,13},{6,14},{7,15},{8,0},{9,1},... | collective-permute-start | bytes 786440 | tf_op jit(solution)/shard_map/ppermute | solution.py:711
  143.3 18.3 %collective-permute-start.39 = (bf16[576,256]{1,0:T(8,128)(2,1)S(1)}, bf16[576,256]{1,0:T(8,128)(2,1)S(1)}, u32[]{:S(2)}, u32[]{:S(2)}) collective-permute-start(bf16[576,256]{1,0:T(8,128)(2,1)S(1)} %pad_maximum_fusion.6), channel_id=1, source_target_pairs={{0,4},{1,9},{2,6},{3,11},{4,0},{5,13},{6,2},{7,15},{8,12},{9,1},{1... | collective-permute-start | bytes 884744 | tf_op jit(solution)/shard_map/ppermute | solution.py:711
  155.6 14.1 %collective-permute-start.43 = (bf16[192,256]{1,0:T(8,128)(2,1)S(1)}, bf16[192,256]{1,0:T(8,128)(2,1)S(1)}, u32[]{:S(2)}, u32[]{:S(2)}) collective-permute-start(bf16[192,256]{1,0:T(8,128)(2,1)S(1)} %pad_maximum_fusion.11), channel_id=1, source_target_pairs={{0,2},{1,3},{2,0},{3,1},{4,6},{5,7},{6,4},{7,5},{8,10},{9,11},{10,... | collective-permute-start | bytes 294920 | tf_op jit(solution)/shard_map/ppermute | solution.py:711
  161.7 15.3 %collective-permute-start.50 = (bf16[1152,256]{1,0:T(8,128)(2,1)S(1)}, bf16[1152,256]{1,0:T(8,128)(2,1)S(1)}, u32[]{:S(2)}, u32[]{:S(2)}) collective-permute-start(bf16[1152,256]{1,0:T(8,128)(2,1)S(1)} %pad_maximum_fusion.2), channel_id=1, source_target_pairs={{0,2},{1,5},{2,0},{3,7},{4,6},{5,1},{6,4},{7,3},{8,10},{9,13},{10,... | collective-permute-start | bytes 1769480 | tf_op jit(solution)/shard_map/ppermute | solution.py:711
  169.7 16.1 %collective-permute-start.23 = (f32[1024,256]{1,0:T(8,128)S(1)}, f32[1024,256]{1,0:T(8,128)S(1)}, u32[]{:S(2)}, u32[]{:S(2)}) collective-permute-start(f32[1024,256]{1,0:T(8,128)S(1)} %get-tuple-element.219), channel_id=1, source_target_pairs={{0,1},{1,0},{2,3},{3,2},{4,5},{5,4},{6,7},{7,6},{8,9},{9,8},{10,11... | collective-permute-start | bytes 3145736 | tf_op jit(solution)/shard_map/ppermute | solution.py:828
  169.7 18.4 %collective-permute-start.24 = (f32[1024,256]{1,0:T(8,128)S(1)}, f32[1024,256]{1,0:T(8,128)S(1)}, u32[]{:S(2)}, u32[]{:S(2)}) collective-permute-start(f32[1024,256]{1,0:T(8,128)S(1)} %get-tuple-element.221), channel_id=1, source_target_pairs={{0,1},{1,0},{2,3},{3,2},{4,5},{5,4},{6,7},{7,6},{8,9},{9,8},{10,11... | collective-permute-start | bytes 3145736 | tf_op jit(solution)/shard_map/ppermute | solution.py:828
  177.0 14.9 %collective-permute-start.53 = (bf16[1024,256]{1,0:T(8,128)(2,1)S(1)}, bf16[1024,256]{1,0:T(8,128)(2,1)S(1)}, u32[]{:S(2)}, u32[]{:S(2)}) collective-permute-start(bf16[1024,256]{1,0:T(8,128)(2,1)S(1)} %pad_maximum_fusion.3.refs_0_), channel_id=1, source_target_pairs={{0,4},{1,5},{2,6},{3,7},{4,0},{5,1},{6,2},{7,3},{8,12},{9,13},{10,... | collective-permute-start | bytes 1572872 | tf_op jit(solution)/shard_map/ppermute | solution.py:711
  183.0 28.9 %collective-permute-start.51 = (bf16[2304,256]{1,0:T(8,128)(2,1)S(1)}, bf16[2304,256]{1,0:T(8,128)(2,1)S(1)}, u32[]{:S(2)}, u32[]{:S(2)}) collective-permute-start(bf16[2304,256]{1,0:T(8,128)(2,1)S(1)} %pad_maximum_fusion.refs_0_), channel_id=1, source_target_pairs={{0,8},{1,3},{2,10},{3,1},{4,12},{5,7},{6,14},{7,5},{8,0},{9,11},{1... | collective-permute-start | bytes 3538952 | tf_op jit(solution)/shard_map/ppermute | solution.py:711
  184.5 23.1 %collective-permute-start.49 = (bf16[1536,256]{1,0:T(8,128)(2,1)S(1)}, bf16[1536,256]{1,0:T(8,128)(2,1)S(1)}, u32[]{:S(2)}, u32[]{:S(2)}) collective-permute-start(bf16[1536,256]{1,0:T(8,128)(2,1)S(1)} %pad_maximum_fusion.1.refs_1_), channel_id=1, source_target_pairs={{0,8},{1,3},{2,10},{3,1},{4,12},{5,7},{6,14},{7,5},{8,0},{9,11},{1... | collective-permute-start | bytes 2359304 | tf_op jit(solution)/shard_map/ppermute | solution.py:711
  185.8 14.5 %collective-permute-start.45 = (bf16[768,256]{1,0:T(8,128)(2,1)S(1)}, bf16[768,256]{1,0:T(8,128)(2,1)S(1)}, u32[]{:S(2)}, u32[]{:S(2)}) collective-permute-start(bf16[768,256]{1,0:T(8,128)(2,1)S(1)} %pad_maximum_fusion.4.refs_0_), channel_id=1, source_target_pairs={{0,4},{1,5},{2,6},{3,7},{4,0},{5,1},{6,2},{7,3},{8,12},{9,13},{10,... | collective-permute-start | bytes 1179656 | tf_op jit(solution)/shard_map/ppermute | solution.py:711
  (47 other events, 305.5 us)

commit v2 on v1

--- a/solution.py
+++ b/solution.py
@@ -694,10 +694,10 @@
 
 EVERY, TIED, SMALL_FROM = "asrf", 9, 0
 ORDERS = {
-    "second": ((2, 0, 1), (0, 1, 2)),
-    "attn": ((1, 2, 0), (1, 2, 0)),
-    "first": ((2, 0, 1), (0, 1, 2)),
-    "rest": ((1, 2, 0), (1, 2, 0)),
+    "second": ((0, 2, 1), (2, 1, 0)),
+    "attn": ((1, 0, 2), (1, 2, 0)),
+    "first": ((0, 2, 1), (1, 0, 2)),
+    "rest": ((2, 1, 0), (2, 1, 0)),
 }
 
 

time: 215 us -> 223 us (1.037)
  other arithmetic: 6.53 us -> 12.8 us
  waiting for transfers between devices: 52.6 us -> 56.1 us
    concatenate x12, other arithmetic: 0.34 us -> 6.62 us  [advance(): jnp.concatenate([self.value, back], 0)]
    ppermute x32, starting transfers between devices: 43.1 us -> 37.1 us  [exchange(): lax.ppermute(array, ('dp', 'chan'), [(a[0] * 2 + a[1], b[0] * 2 + b[1]) f...]
    ppermute x4, starting transfers between devices: 3.85 us -> 8.06 us  [shards(): lax.ppermute(small, 'dp', [(i, i ^ 1 << bit) for i in range(size)])]
    ppermute x4, waiting for transfers between devices: 2.28 us -> 6.15 us  [shards(): lax.ppermute(small, 'dp', [(i, i ^ 1 << bit) for i in range(size)])]
  transfers between devices with their start and end apart: 54 -> 54, of which waited for: 17 -> 16; matrix products, arithmetic and copies ran while one was open for 4% -> 7% of each run, Pallas kernels for 43% -> 42%
where the time goes in v2:
time: 223 us
  Pallas kernels  95.6 us (43%)
  waiting for transfers between devices  56.1 us (25%)
  starting transfers between devices  49.8 us (22%)
  other arithmetic  12.8 us (6%)
  local copies, waits for them, and re-layouts  7.19 us (3%)
    ppermute x32, waiting for transfers between devices, exchange(): lax.ppermute(array, ('dp', 'chan'), [(a[0] * 2 + a[1], b[0] * 2 + b[1]) f...  47.5 us
    ppermute x32, starting transfers between devices, exchange(): lax.ppermute(array, ('dp', 'chan'), [(a[0] * 2 + a[1], b[0] * 2 + b[1]) f...  37.1 us
    pallas_call x1, Pallas kernels, attn_call(): pl.pallas_call(attn_kernel, out_shape=(shape(PIX, HALF, F32), shape(PIX,...  27.2 us
    pallas_call x2, Pallas kernels, dgrad_call(): pl.pallas_call(functools.partial(dgrad_kernel, first), out_shape=outs + (...  22.7 us
    pallas_call x1, Pallas kernels, front_call(): pl.pallas_call(front_kernel, out_shape=(half, half, shape(8, HALF, F32),...  10.3 us
    pallas_call x1, Pallas kernels, wgrad1_call(): pl.pallas_call(wgrad1_kernel, out_shape=(shape(TAPS * C, HALF, BF), shape...  8.24 us
    ppermute x4, starting transfers between devices, shards(): lax.ppermute(small, 'dp', [(i, i ^ 1 << bit) for i in range(size)])  8.06 us
    pallas_call x1, Pallas kernels, wgrad2_call(): pl.pallas_call(wgrad2_kernel, out_shape=shape(9 * C, HALF, BF), in_specs=...  8.01 us
  transfers between devices with their start and end apart: 54, of which 16 were waited for; matrix products, arithmetic and copies ran while one was open for 7% of the time, Pallas kernels for 42%

profile of v2, /device:TPU:0, one launch (start us, length us, event | category | flops | bytes accessed | tf_op | source)
XLA Modules:
  0.0 222.9 jit_solution(2399523387160944633)
XLA Ops:
  6.5 10.3 %front.1 = (bf16[1024,256]{1,0:T(8,128)(2,1)}, bf16[1024,256]{1,0:T(8,128)(2,1)}, f32[8,256]{1,0:T(8,128)S(1)}, f32[8,256]{1,0:T(8,128)S(1)}, bf16[2,576,1536]{2...) custom-call(s32[1]{0:T(128)} %bitcast.core_ref, ...), custom_call_target="tpu_custom_call" | custom-call | flops 9900000256 | bytes 1048576 | tf_op jit(solution)/shard_map/front/pallas_call | solution.py:351
  18.4 6.5 %front_peer.1 = (f32[1024,256]{1,0:T(8,128)}, bf16[1024,256]{1,0:T(8,128)(2,1)S(1)}, f32[8,256]{1,0:T(8,128)S(1)}) custom-call(s32[1]{0:T(128)} %bitcast.core_ref, f32[16]{0:T(128)S(1)} %slice_bitcast_fusion.eq_ref, bf16[2,576,1536]{2,1,0:T(8,128)(2,1)S(1)} %get-tuple-element.159.band, bf16[9,512,256]{2,1,0:T(8,128)(2,1)} %copy-done.5, ...), custom_call_target="tpu_custom_call" | custom-call | flops 5500000256 | bytes 1048576 | tf_op jit(solution)/shard_map/front_peer/pallas_call | solution.py:366
  26.7 27.2 %attention.1 = (f32[1024,256]{1,0:T(8,128)S(1)}, f32[1024,256]{1,0:T(8,128)S(1)}, f32[1024,512]{1,0:T(8,128)}, bf16[1024,512]{1,0:T(8,128)(2,1)}, f32[8,512]{1,0...) custom-call(s32[1]{0:T(128)} %bitcast.core_ref, ...), custom_call_target="tpu_custom_call" | custom-call | flops 30799998976 | bytes 1048576 | tf_op jit(solution)/shard_map/attention/pallas_call | solution.py:483
  54.8 4.3 %attention_weights.1 = (bf16[2048,256]{1,0:T(8,128)(2,1)S(1)}, bf16[2048,256]{1,0:T(8,128)(2,1)}) custom-call(s32[1]{0:T(128)} %bitcast.core_ref, bf16[1024,512]{1,0:T(8,128)(2,1)S(1)} %get-tuple-element.172.normed_ref, bf16[1024,512]{1,0:T(8,128)(2,1)S(1)} %get-tuple-element.173.dquery, bf16[1024,512]{1,0:T(8,128)(2,1)S(1)} %get-tuple-element.174.dkey, ...), custom_call_target="tpu_custom_call" | custom-call | flops 3300000000 | bytes 1048576 | tf_op jit(solution)/shard_map/attention_weights/pallas_call | solution.py:520
  59.5 8.0 %wgrad2.1 = bf16[4608,256]{1,0:T(8,128)(2,1)S(1)} custom-call(s32[1]{0:T(128)} %bitcast.core_ref, f32[2,16]{1,0:T(2,128)S(1)} %broadcast_select_fusion.eq_ref, bf16[1024,256]{1,0:T(8,128)(2,1)} %copy-done.1, bf16[1024,256]{1,0:T(8,128)(2,1)} %copy-done.12, bf16[1024,512]{1,0:T(8,128)(2,1)} %get-tuple-element.191.refs_2_.refs_0_, ...), custom_call_target="tpu_custom_call" | custom-call | flops 7699999744 | bytes 1048576 | tf_op jit(solution)/shard_map/wgrad2/pallas_call | solution.py:565
  69.2 2.7 %collective-permute-start.14 = (bf16[2304,256]{1,0:T(8,128)(2,1)S(1)}, bf16[2304,256]{1,0:T(8,128)(2,1)S(1)}, u32[]{:S(2)}, u32[]{:S(2)}) collective-permute-start(bf16[2304,256]{1,0:T(8,128)(2,1)S(1)} %constant_dynamic-slice_fusion.15), channel_id=1, source_target_pairs={{0,2},{1,9},{2,0},{3,11},{4,6},{5,13},{6,4},{7,15},{8,10},{9,1},{1... | collective-permute-start | bytes 3538952 | tf_op jit(solution)/shard_map/ppermute | solution.py:711
  73.5 11.5 %dgrad2.1 = (bf16[1024,256]{1,0:T(8,128)(2,1)S(1)}, bf16[1024,256]{1,0:T(8,128)(2,1)S(1)}, f32[8,512]{1,0:T(8,128)S(1)}) custom-call(s32[1]{0:T(128)} %bitcast.core_ref, f32[16]{0:T(128)S(1)} %slice_bitcast_fusion.eq_ref, bf16[9,256,512]{2,1,0:T(8,128)(2,1)} %own_ref.1, bf16[9,256,512]{2,1,0:T(8,128)(2,1)} %copy-done.6, ...), custom_call_target="tpu_custom_call" | custom-call | flops 11000000512 | bytes 1048576 | tf_op jit(solution)/shard_map/dgrad2/pallas_call | solution.py:683
  90.2 8.2 %wgrad1.1 = (bf16[3072,256]{1,0:T(8,128)(2,1)S(1)}, bf16[1536,256]{1,0:T(8,128)(2,1)S(1)}) custom-call(s32[1]{0:T(128)} %bitcast.core_ref, f32[2,16]{1,0:T(2,128)S(1)} %broadcast_select_fusion.eq_ref, bf16[1024,256]{1,0:T(8,128)(2,1)} %copy-done.2, bf16[1024,256]{1,0:T(8,128)(2,1)} %copy-done.13, bf16[1024,256]{1,0:T(8,128)(2,1)} %get-tuple-element.180.refs_2_, ...), custom_call_target="tpu_custom_call" | custom-call | flops 7699999744 | bytes 1048576 | tf_op jit(solution)/shard_map/wgrad1/pallas_call | solution.py:613
  105.4 11.2 %dgrad1.1 = (f32[1024,256]{1,0:T(8,128)S(1)}, f32[1024,256]{1,0:T(8,128)S(1)}, f32[8,512]{1,0:T(8,128)S(1)}) custom-call(s32[1]{0:T(128)} %bitcast.core_ref, f32[16]{0:T(128)S(1)} %slice_bitcast_fusion.eq_ref, bf16[9,512,256]{2,1,0:T(8,128)(2,1)} %own_ref.2, bf16[9,512,256]{2,1,0:T(8,128)(2,1)} %copy-done.5, ...), custom_call_target="tpu_custom_call" | custom-call | flops 11000000512 | bytes 1048576 | tf_op jit(solution)/shard_map/dgrad1/pallas_call | solution.py:683
  118.2 2.6 %collective-permute-start.30 = (bf16[128,256]{1,0:T(8,128)(2,1)S(1)}, bf16[128,256]{1,0:T(8,128)(2,1)S(1)}, u32[]{:S(2)}, u32[]{:S(2)}) collective-permute-start(bf16[128,256]{1,0:T(8,128)(2,1)S(1)} %constant_dynamic-slice_fusion.4), channel_id=1, source_target_pairs={{0,16},{1,17},{2,18},{3,19},{4,20},{5,21},{6,22},{7,23},{8,24},{9,... | collective-permute-start | bytes 196616 | tf_op jit(solution)/shard_map/ppermute | solution.py:711
  122.0 2.6 %collective-permute-done.26 = f32[24,256]{1,0:T(8,128)S(1)} collective-permute-done((f32[24,256]{1,0:T(8,128)S(1)}, f32[24,256]{1,0:T(8,128)S(1)}, u32[]{:S(2)}, u32[]{:S(2)}) %collective-permute-start.26) | collective-permute-done | bytes 24608 | tf_op jit(solution)/shard_map/ppermute | solution.py:914
  128.5 5.1 %collective-permute-start.36 = (f32[24,256]{1,0:T(8,128)S(1)}, f32[24,256]{1,0:T(8,128)S(1)}, u32[]{:S(2)}, u32[]{:S(2)}) collective-permute-start(f32[24,256]{1,0:T(8,128)S(1)} %add.243), channel_id=1, source_target_pairs={{0,8},{2,10},{4,12},{6,14},{8,0},{10,2},{12,4},{14,6},{16,24},{18,... | collective-permute-start | bytes 73736 | tf_op jit(solution)/shard_map/ppermute | solution.py:914
  137.8 2.8 %collective-permute-start.34 = (bf16[288,256]{1,0:T(8,128)(2,1)S(1)}, bf16[288,256]{1,0:T(8,128)(2,1)S(1)}, u32[]{:S(2)}, u32[]{:S(2)}) collective-permute-start(bf16[288,256]{1,0:T(8,128)(2,1)S(1)} %dynamic-slice_add_fusion.10), channel_id=1, source_target_pairs={{0,16},{1,17},{2,18},{3,19},{4,20},{5,21},{6,22},{7,23},{8,24},{9,... | collective-permute-start | bytes 442376 | tf_op jit(solution)/shard_map/ppermute | solution.py:711
  140.8 7.9 %collective-permute-done.40 = bf16[256,256]{1,0:T(8,128)(2,1)S(1)} collective-permute-done((bf16[256,256]{1,0:T(8,128)(2,1)S(1)}, bf16[256,256]{1,0:T(8,128)(2,1)S(1)}, u32[]{:S(2)}, u32[]{:S(2)}) %collective-permute-start.40) | collective-permute-done | bytes 131104 | tf_op jit(solution)/shard_map/ppermute | solution.py:711
  151.3 2.7 %collective-permute-done.38 = bf16[96,256]{1,0:T(8,128)(2,1)S(1)} collective-permute-done((bf16[96,256]{1,0:T(8,128)(2,1)S(1)}, bf16[96,256]{1,0:T(8,128)(2,1)S(1)}, u32[]{:S(2)}, u32[]{:S(2)}) %collective-permute-start.38) | collective-permute-done | bytes 49184 | tf_op jit(solution)/shard_map/ppermute | solution.py:711
  154.3 3.6 %collective-permute-done.32 = bf16[384,256]{1,0:T(8,128)(2,1)S(1)} collective-permute-done((bf16[384,256]{1,0:T(8,128)(2,1)S(1)}, bf16[384,256]{1,0:T(8,128)(2,1)S(1)}, u32[]{:S(2)}, u32[]{:S(2)}) %collective-permute-start.32) | collective-permute-done | bytes 196640 | tf_op jit(solution)/shard_map/ppermute | solution.py:711
  158.0 3.0 %collective-permute-start.37 = (bf16[192,256]{1,0:T(8,128)(2,1)S(1)}, bf16[192,256]{1,0:T(8,128)(2,1)S(1)}, u32[]{:S(2)}, u32[]{:S(2)}) collective-permute-start(bf16[192,256]{1,0:T(8,128)(2,1)S(1)} %constant_dynamic-slice_fusion.1), channel_id=1, source_target_pairs={{0,16},{1,17},{2,18},{3,19},{4,20},{5,21},{6,22},{7,23},{8,24},{9,... | collective-permute-start | bytes 294920 | tf_op jit(solution)/shard_map/ppermute | solution.py:711
  167.4 3.2 %collective-permute-done.46 = bf16[192,256]{1,0:T(8,128)(2,1)S(1)} collective-permute-done((bf16[192,256]{1,0:T(8,128)(2,1)S(1)}, bf16[192,256]{1,0:T(8,128)(2,1)S(1)}, u32[]{:S(2)}, u32[]{:S(2)}) %collective-permute-start.46) | collective-permute-done | bytes 98336 | tf_op jit(solution)/shard_map/ppermute | solution.py:711
  173.8 4.1 %collective-permute-done.47 = bf16[384,256]{1,0:T(8,128)(2,1)} collective-permute-done((bf16[384,256]{1,0:T(8,128)(2,1)}, bf16[384,256]{1,0:T(8,128)(2,1)}, u32[]{:S(2)}, u32[]{:S(2)}) %collective-permute-start.47) | collective-permute-done | bytes 196640 | tf_op jit(solution)/shard_map/ppermute | solution.py:711
  183.4 6.0 %collective-permute-done.48 = bf16[768,256]{1,0:T(8,128)(2,1)S(1)} collective-permute-done((bf16[768,256]{1,0:T(8,128)(2,1)S(1)}, bf16[768,256]{1,0:T(8,128)(2,1)S(1)}, u32[]{:S(2)}, u32[]{:S(2)}) %collective-permute-start.48) | collective-permute-done | bytes 393248 | tf_op jit(solution)/shard_map/ppermute | solution.py:711
  189.4 3.9 %collective-permute-start.51 = (bf16[2304,256]{1,0:T(8,128)(2,1)S(1)}, bf16[2304,256]{1,0:T(8,128)(2,1)S(1)}, u32[]{:S(2)}, u32[]{:S(2)}) collective-permute-start(bf16[2304,256]{1,0:T(8,128)(2,1)S(1)} %pad_maximum_fusion.refs_0_), channel_id=1, source_target_pairs={{0,2},{1,9},{2,0},{3,11},{4,6},{5,13},{6,4},{7,15},{8,10},{9,1},{1... | collective-permute-start | bytes 3538952 | tf_op jit(solution)/shard_map/ppermute | solution.py:711
  198.6 7.7 %collective-permute-done.45.refs_0_ = bf16[768,256]{1,0:T(8,128)(2,1)S(1)} collective-permute-done((bf16[768,256]{1,0:T(8,128)(2,1)S(1)}, bf16[768,256]{1,0:T(8,128)(2,1)S(1)}, u32[]{:S(2)}, u32[]{:S(2)}) %collective-permute-start.45) | collective-permute-done | bytes 393248 | tf_op jit(solution)/shard_map/ppermute | solution.py:711
  206.3 9.7 %collective-permute-done.49.refs_1_ = bf16[1536,256]{1,0:T(8,128)(2,1)S(1)} collective-permute-done((bf16[1536,256]{1,0:T(8,128)(2,1)S(1)}, bf16[1536,256]{1,0:T(8,128)(2,1)S(1)}, u32[]{:S(2)}, u32[]{:S(2)}) %collective-permute-start.49) | collective-permute-done | bytes 786464 | tf_op jit(solution)/shard_map/ppermute | solution.py:711
  220.2 2.7 %place.2 = f32[2304,512]{1,0:T(8,128)} custom-call(s32[1]{0:T(128)} %bitcast.25.base_ref, bf16[2304,256]{1,0:T(8,128)(2,1)S(1)} %pad_maximum_fusion.refs_0_, bf16[2304,256]{1,0:T(8,128)(2,1)S(1)} %collective-permute-done.51.refs_1_), custom_call_target="tpu_custom_call" | custom-call | flops 2200000000 | bytes 1048576 | tf_op jit(solution)/shard_map/place/pallas_call | solution.py:819
  (199 shorter events, 64.1 us)
Async XLA Ops:
  17.5 36.4 %collective-permute-start.11 = (bf16[1024,256]{1,0:T(8,128)(2,1)}, bf16[1024,256]{1,0:T(8,128)(2,1)S(1)}, u32[]{:S(2)}, u32[]{:S(2)}) collective-permute-start(bf16[1024,256]{1,0:T(8,128)(2,1)} %get-tuple-element.179.refs_3_), channel_id=1, source_target_pairs={{0,1},{1,0},{2,3},{3,2},{4,5},{5,4},{6,7},{7,6},{8,9},{9,8},{10,11... | collective-permute-start | bytes 1572872 | tf_op jit(solution)/shard_map/ppermute | solution.py:828
  17.8 36.1 %collective-permute-start.12 = (bf16[1024,256]{1,0:T(8,128)(2,1)}, bf16[1024,256]{1,0:T(8,128)(2,1)S(1)}, u32[]{:S(2)}, u32[]{:S(2)}) collective-permute-start(bf16[1024,256]{1,0:T(8,128)(2,1)} %get-tuple-element.180.refs_2_), channel_id=1, source_target_pairs={{0,1},{1,0},{2,3},{3,2},{4,5},{5,4},{6,7},{7,6},{8,9},{9,8},{10,11... | collective-permute-start | bytes 1572872 | tf_op jit(solution)/shard_map/ppermute | solution.py:828
  25.0 28.9 %collective-permute-start.10 = (bf16[1024,256]{1,0:T(8,128)(2,1)S(1)}, bf16[1024,256]{1,0:T(8,128)(2,1)S(1)}, u32[]{:S(2)}, u32[]{:S(2)}) collective-permute-start(bf16[1024,256]{1,0:T(8,128)(2,1)S(1)} %get-tuple-element.164.act_peer), channel_id=1, source_target_pairs={{0,1},{1,0},{2,3},{3,2},{4,5},{5,4},{6,7},{7,6},{8,9},{9,8},{10,11... | collective-permute-start | bytes 1572872 | tf_op jit(solution)/shard_map/ppermute | solution.py:828
  69.2 17.0 %collective-permute-start.14 = (bf16[2304,256]{1,0:T(8,128)(2,1)S(1)}, bf16[2304,256]{1,0:T(8,128)(2,1)S(1)}, u32[]{:S(2)}, u32[]{:S(2)}) collective-permute-start(bf16[2304,256]{1,0:T(8,128)(2,1)S(1)} %constant_dynamic-slice_fusion.15), channel_id=1, source_target_pairs={{0,2},{1,9},{2,0},{3,11},{4,6},{5,13},{6,4},{7,15},{8,10},{9,1},{1... | collective-permute-start | bytes 3538952 | tf_op jit(solution)/shard_map/ppermute | solution.py:711
  71.9 14.1 %collective-permute-start.15 = (bf16[1024,256]{1,0:T(8,128)(2,1)S(1)}, bf16[1024,256]{1,0:T(8,128)(2,1)S(1)}, u32[]{:S(2)}, u32[]{:S(2)}) collective-permute-start(bf16[1024,256]{1,0:T(8,128)(2,1)S(1)} %constant_dynamic-slice_fusion.14), channel_id=1, source_target_pairs={{0,4},{1,5},{2,6},{3,7},{4,0},{5,1},{6,2},{7,3},{8,12},{9,13},{10,... | collective-permute-start | bytes 1572872 | tf_op jit(solution)/shard_map/ppermute | solution.py:711
  87.8 12.2 %collective-permute-start.17 = (bf16[1152,256]{1,0:T(8,128)(2,1)S(1)}, bf16[1152,256]{1,0:T(8,128)(2,1)S(1)}, u32[]{:S(2)}, u32[]{:S(2)}) collective-permute-start(bf16[1152,256]{1,0:T(8,128)(2,1)S(1)} %constant_dynamic-slice_fusion.13), channel_id=1, source_target_pairs={{0,8},{1,5},{2,10},{3,7},{4,12},{5,1},{6,14},{7,3},{8,0},{9,13},{1... | collective-permute-start | bytes 1769480 | tf_op jit(solution)/shard_map/ppermute | solution.py:711
  100.2 16.4 %collective-permute-start.19 = (bf16[256,256]{1,0:T(8,128)(2,1)S(1)}, bf16[256,256]{1,0:T(8,128)(2,1)S(1)}, u32[]{:S(2)}, u32[]{:S(2)}) collective-permute-start(bf16[256,256]{1,0:T(8,128)(2,1)S(1)} %constant_dynamic-slice_fusion.11), channel_id=1, source_target_pairs={{0,8},{1,3},{2,10},{3,1},{4,12},{5,7},{6,14},{7,5},{8,0},{9,11},{1... | collective-permute-start | bytes 393224 | tf_op jit(solution)/shard_map/ppermute | solution.py:711
  101.9 14.8 %collective-permute-start.20 = (bf16[576,256]{1,0:T(8,128)(2,1)S(1)}, bf16[576,256]{1,0:T(8,128)(2,1)S(1)}, u32[]{:S(2)}, u32[]{:S(2)}) collective-permute-start(bf16[576,256]{1,0:T(8,128)(2,1)S(1)} %constant_dynamic-slice_fusion.10), channel_id=1, source_target_pairs={{0,4},{1,3},{2,6},{3,1},{4,0},{5,7},{6,2},{7,5},{8,12},{9,11},{10,... | collective-permute-start | bytes 884744 | tf_op jit(solution)/shard_map/ppermute | solution.py:711
  103.2 13.5 %collective-permute-start.21 = (bf16[768,256]{1,0:T(8,128)(2,1)S(1)}, bf16[768,256]{1,0:T(8,128)(2,1)S(1)}, u32[]{:S(2)}, u32[]{:S(2)}) collective-permute-start(bf16[768,256]{1,0:T(8,128)(2,1)S(1)} %constant_dynamic-slice_fusion.9), channel_id=1, source_target_pairs={{0,8},{1,9},{2,10},{3,11},{4,12},{5,13},{6,14},{7,15},{8,0},{9,1},... | collective-permute-start | bytes 1179656 | tf_op jit(solution)/shard_map/ppermute | solution.py:711
  103.8 13.1 %collective-permute-start.22 = (bf16[1536,256]{1,0:T(8,128)(2,1)S(1)}, bf16[1536,256]{1,0:T(8,128)(2,1)S(1)}, u32[]{:S(2)}, u32[]{:S(2)}) collective-permute-start(bf16[1536,256]{1,0:T(8,128)(2,1)S(1)} %constant_dynamic-slice_fusion.8), channel_id=1, source_target_pairs={{0,2},{1,5},{2,0},{3,7},{4,6},{5,1},{6,4},{7,3},{8,10},{9,13},{10,... | collective-permute-start | bytes 2359304 | tf_op jit(solution)/shard_map/ppermute | solution.py:711
  117.6 23.0 %collective-permute-start.28 = (bf16[384,256]{1,0:T(8,128)(2,1)S(1)}, bf16[384,256]{1,0:T(8,128)(2,1)S(1)}, u32[]{:S(2)}, u32[]{:S(2)}) collective-permute-start(bf16[384,256]{1,0:T(8,128)(2,1)S(1)} %constant_dynamic-slice_fusion.6), channel_id=1, source_target_pairs={{0,4},{1,5},{2,6},{3,7},{4,0},{5,1},{6,2},{7,3},{8,12},{9,13},{10,... | collective-permute-start | bytes 589832 | tf_op jit(solution)/shard_map/ppermute | solution.py:711
  121.6 16.1 %collective-permute-start.29 = (bf16[288,256]{1,0:T(8,128)(2,1)S(1)}, bf16[288,256]{1,0:T(8,128)(2,1)S(1)}, u32[]{:S(2)}, u32[]{:S(2)}) collective-permute-start(bf16[288,256]{1,0:T(8,128)(2,1)S(1)} %constant_dynamic-slice_fusion.5), channel_id=1, source_target_pairs={{0,16},{1,17},{2,18},{3,19},{4,20},{5,21},{6,22},{7,23},{8,24},{9,... | collective-permute-start | bytes 442376 | tf_op jit(solution)/shard_map/ppermute | solution.py:711
  133.6 17.4 %collective-permute-start.27 = (bf16[768,256]{1,0:T(8,128)(2,1)S(1)}, bf16[768,256]{1,0:T(8,128)(2,1)S(1)}, u32[]{:S(2)}, u32[]{:S(2)}) collective-permute-start(bf16[768,256]{1,0:T(8,128)(2,1)S(1)} %constant_dynamic-slice_fusion.7), channel_id=1, source_target_pairs={{0,8},{1,3},{2,10},{3,1},{4,12},{5,7},{6,14},{7,5},{8,0},{9,11},{1... | collective-permute-start | bytes 1179656 | tf_op jit(solution)/shard_map/ppermute | solution.py:711
  135.4 36.9 %collective-permute-start.41 = (f32[24,256]{1,0:T(8,128)S(1)}, f32[24,256]{1,0:T(8,128)S(1)}, u32[]{:S(2)}, u32[]{:S(2)}) collective-permute-start(f32[24,256]{1,0:T(8,128)S(1)} %add.250), channel_id=1, source_target_pairs={{0,16},{2,18},{4,20},{6,22},{8,24},{10,26},{12,28},{14,30},{16,0},... | collective-permute-start | bytes 73736 | tf_op jit(solution)/shard_map/ppermute | solution.py:914
  136.0 12.7 %collective-permute-start.40 = (bf16[256,256]{1,0:T(8,128)(2,1)S(1)}, bf16[256,256]{1,0:T(8,128)(2,1)S(1)}, u32[]{:S(2)}, u32[]{:S(2)}) collective-permute-start(bf16[256,256]{1,0:T(8,128)(2,1)S(1)} %pad_maximum_fusion.10), channel_id=1, source_target_pairs={{0,8},{1,3},{2,10},{3,1},{4,12},{5,7},{6,14},{7,5},{8,0},{9,11},{1... | collective-permute-start | bytes 393224 | tf_op jit(solution)/shard_map/ppermute | solution.py:711
  148.7 30.9 %collective-permute-start.52 = (bf16[512,256]{1,0:T(8,128)(2,1)S(1)}, bf16[512,256]{1,0:T(8,128)(2,1)}, u32[]{:S(2)}, u32[]{:S(2)}) collective-permute-start(bf16[512,256]{1,0:T(8,128)(2,1)S(1)} %pad_maximum_fusion.7), channel_id=1, source_target_pairs={{0,2},{1,9},{2,0},{3,11},{4,6},{5,13},{6,4},{7,15},{8,10},{9,1},{1... | collective-permute-start | bytes 786440 | tf_op jit(solution)/shard_map/ppermute | solution.py:711
  149.0 17.6 %collective-permute-start.39 = (bf16[576,256]{1,0:T(8,128)(2,1)S(1)}, bf16[576,256]{1,0:T(8,128)(2,1)S(1)}, u32[]{:S(2)}, u32[]{:S(2)}) collective-permute-start(bf16[576,256]{1,0:T(8,128)(2,1)S(1)} %pad_maximum_fusion.6), channel_id=1, source_target_pairs={{0,4},{1,3},{2,6},{3,1},{4,0},{5,7},{6,2},{7,5},{8,12},{9,11},{10,... | collective-permute-start | bytes 884744 | tf_op jit(solution)/shard_map/ppermute | solution.py:711
  167.4 13.8 %collective-permute-start.50 = (bf16[1152,256]{1,0:T(8,128)(2,1)}, bf16[1152,256]{1,0:T(8,128)(2,1)}, u32[]{:S(2)}, u32[]{:S(2)}) collective-permute-start(bf16[1152,256]{1,0:T(8,128)(2,1)} %pad_maximum_fusion.2), channel_id=1, source_target_pairs={{0,8},{1,5},{2,10},{3,7},{4,12},{5,1},{6,14},{7,3},{8,0},{9,13},{1... | collective-permute-start | bytes 1769480 | tf_op jit(solution)/shard_map/ppermute | solution.py:711
  172.3 21.9 %collective-permute-start.23 = (f32[1024,256]{1,0:T(8,128)S(1)}, f32[1024,256]{1,0:T(8,128)S(1)}, u32[]{:S(2)}, u32[]{:S(2)}) collective-permute-start(f32[1024,256]{1,0:T(8,128)S(1)} %get-tuple-element.219), channel_id=1, source_target_pairs={{0,1},{1,0},{2,3},{3,2},{4,5},{5,4},{6,7},{7,6},{8,9},{9,8},{10,11... | collective-permute-start | bytes 3145736 | tf_op jit(solution)/shard_map/ppermute | solution.py:828
  172.3 23.4 %collective-permute-start.24 = (f32[1024,256]{1,0:T(8,128)}, f32[1024,256]{1,0:T(8,128)S(1)}, u32[]{:S(2)}, u32[]{:S(2)}) collective-permute-start(f32[1024,256]{1,0:T(8,128)} %copy-done), channel_id=1, source_target_pairs={{0,1},{1,0},{2,3},{3,2},{4,5},{5,4},{6,7},{7,6},{8,9},{9,8},{10,11... | collective-permute-start | bytes 3145736 | tf_op jit(solution)/shard_map/ppermute | solution.py:828
  177.9 15.5 %collective-permute-start.44 = (bf16[384,256]{1,0:T(8,128)(2,1)S(1)}, bf16[384,256]{1,0:T(8,128)(2,1)S(1)}, u32[]{:S(2)}, u32[]{:S(2)}) collective-permute-start(bf16[384,256]{1,0:T(8,128)(2,1)S(1)} %pad_maximum_fusion.8), channel_id=1, source_target_pairs={{0,4},{1,5},{2,6},{3,7},{4,0},{5,1},{6,2},{7,3},{8,12},{9,13},{10,... | collective-permute-start | bytes 589832 | tf_op jit(solution)/shard_map/ppermute | solution.py:711
  181.2 16.0 %collective-permute-start.53 = (bf16[1024,256]{1,0:T(8,128)(2,1)S(1)}, bf16[1024,256]{1,0:T(8,128)(2,1)S(1)}, u32[]{:S(2)}, u32[]{:S(2)}) collective-permute-start(bf16[1024,256]{1,0:T(8,128)(2,1)S(1)} %pad_maximum_fusion.3.refs_0_), channel_id=1, source_target_pairs={{0,4},{1,5},{2,6},{3,7},{4,0},{5,1},{6,2},{7,3},{8,12},{9,13},{10,... | collective-permute-start | bytes 1572872 | tf_op jit(solution)/shard_map/ppermute | solution.py:711
  189.4 30.8 %collective-permute-start.51 = (bf16[2304,256]{1,0:T(8,128)(2,1)S(1)}, bf16[2304,256]{1,0:T(8,128)(2,1)S(1)}, u32[]{:S(2)}, u32[]{:S(2)}) collective-permute-start(bf16[2304,256]{1,0:T(8,128)(2,1)S(1)} %pad_maximum_fusion.refs_0_), channel_id=1, source_target_pairs={{0,2},{1,9},{2,0},{3,11},{4,6},{5,13},{6,4},{7,15},{8,10},{9,1},{1... | collective-permute-start | bytes 3538952 | tf_op jit(solution)/shard_map/ppermute | solution.py:711
  193.4 22.5 %collective-permute-start.49 = (bf16[1536,256]{1,0:T(8,128)(2,1)S(1)}, bf16[1536,256]{1,0:T(8,128)(2,1)S(1)}, u32[]{:S(2)}, u32[]{:S(2)}) collective-permute-start(bf16[1536,256]{1,0:T(8,128)(2,1)S(1)} %pad_maximum_fusion.1.refs_1_), channel_id=1, source_target_pairs={{0,2},{1,5},{2,0},{3,7},{4,6},{5,1},{6,4},{7,3},{8,10},{9,13},{10,... | collective-permute-start | bytes 2359304 | tf_op jit(solution)/shard_map/ppermute | solution.py:711
  (48 other events, 317.6 us)

commit v3 on v1

--- a/solution.py
+++ b/solution.py
@@ -696,7 +696,7 @@
 ORDERS = {
     "second": ((2, 0, 1), (0, 1, 2)),
     "attn": ((1, 2, 0), (1, 2, 0)),
-    "first": ((2, 0, 1), (0, 1, 2)),
+    "first": ((0, 1, 2), (2, 0, 1)),
     "rest": ((1, 2, 0), (1, 2, 0)),
 }
 

time: 215 us -> 212 us (0.986)
  waiting for transfers between devices: 52.6 us -> 44.3 us
  other arithmetic: 6.53 us -> 12.8 us
    ppermute x32, waiting for transfers between devices: 47.8 us -> 38.8 us  [exchange(): lax.ppermute(array, ('dp', 'chan'), [(a[0] * 2 + a[1], b[0] * 2 + b[1]) f...]
    concatenate x12, other arithmetic: 0.34 us -> 6.62 us  [advance(): jnp.concatenate([self.value, back], 0)]
  transfers between devices with their start and end apart: 54 -> 54, of which waited for: 17 -> 16; matrix products, arithmetic and copies ran while one was open for 4% -> 7% of each run, Pallas kernels for 43% -> 44%
where the time goes in v3:
time: 212 us; the launch traced here: 211 us
  Pallas kernels  95.6 us (45%)
  starting transfers between devices  49.9 us (24%)
  waiting for transfers between devices  44.3 us (21%)
  other arithmetic  12.8 us (6%)
  local copies, waits for them, and re-layouts  7.19 us (3%)
    ppermute x32, starting transfers between devices, exchange(): lax.ppermute(array, ('dp', 'chan'), [(a[0] * 2 + a[1], b[0] * 2 + b[1]) f...  43.1 us
    ppermute x32, waiting for transfers between devices, exchange(): lax.ppermute(array, ('dp', 'chan'), [(a[0] * 2 + a[1], b[0] * 2 + b[1]) f...  38.8 us
    pallas_call x1, Pallas kernels, attn_call(): pl.pallas_call(attn_kernel, out_shape=(shape(PIX, HALF, F32), shape(PIX,...  27.2 us
    pallas_call x2, Pallas kernels, dgrad_call(): pl.pallas_call(functools.partial(dgrad_kernel, first), out_shape=outs + (...  22.7 us
    pallas_call x1, Pallas kernels, front_call(): pl.pallas_call(front_kernel, out_shape=(half, half, shape(8, HALF, F32),...  10.3 us
    pallas_call x1, Pallas kernels, wgrad1_call(): pl.pallas_call(wgrad1_kernel, out_shape=(shape(TAPS * C, HALF, BF), shape...  8.24 us
    pallas_call x1, Pallas kernels, wgrad2_call(): pl.pallas_call(wgrad2_kernel, out_shape=shape(9 * C, HALF, BF), in_specs=...  8.01 us
    concatenate x12, other arithmetic, advance(): jnp.concatenate([self.value, back], 0)  6.62 us
  transfers between devices with their start and end apart: 54, of which 16 were waited for; matrix products, arithmetic and copies ran while one was open for 7% of the time, Pallas kernels for 44%

profile of v3, /device:TPU:0, one launch (start us, length us, event | category | flops | bytes accessed | tf_op | source)
XLA Modules:
  0.0 211.2 jit_solution(630703205085713647)
XLA Ops:
  6.5 10.3 %front.1 = (bf16[1024,256]{1,0:T(8,128)(2,1)}, bf16[1024,256]{1,0:T(8,128)(2,1)}, f32[8,256]{1,0:T(8,128)S(1)}, f32[8,256]{1,0:T(8,128)S(1)}, bf16[2,576,1536]{2...) custom-call(s32[1]{0:T(128)} %bitcast.core_ref, ...), custom_call_target="tpu_custom_call" | custom-call | flops 9900000256 | bytes 1048576 | tf_op jit(solution)/shard_map/front/pallas_call | solution.py:351
  18.4 6.5 %front_peer.1 = (f32[1024,256]{1,0:T(8,128)}, bf16[1024,256]{1,0:T(8,128)(2,1)S(1)}, f32[8,256]{1,0:T(8,128)S(1)}) custom-call(s32[1]{0:T(128)} %bitcast.core_ref, f32[16]{0:T(128)S(1)} %slice_bitcast_fusion.eq_ref, bf16[2,576,1536]{2,1,0:T(8,128)(2,1)S(1)} %get-tuple-element.159.band, bf16[9,512,256]{2,1,0:T(8,128)(2,1)} %copy-done.5, ...), custom_call_target="tpu_custom_call" | custom-call | flops 5500000256 | bytes 1048576 | tf_op jit(solution)/shard_map/front_peer/pallas_call | solution.py:366
  26.7 27.2 %attention.1 = (f32[1024,256]{1,0:T(8,128)S(1)}, f32[1024,256]{1,0:T(8,128)S(1)}, f32[1024,512]{1,0:T(8,128)}, bf16[1024,512]{1,0:T(8,128)(2,1)}, f32[8,512]{1,0...) custom-call(s32[1]{0:T(128)} %bitcast.core_ref, ...), custom_call_target="tpu_custom_call" | custom-call | flops 30799998976 | bytes 1048576 | tf_op jit(solution)/shard_map/attention/pallas_call | solution.py:483
  54.8 4.3 %attention_weights.1 = (bf16[2048,256]{1,0:T(8,128)(2,1)S(1)}, bf16[2048,256]{1,0:T(8,128)(2,1)}) custom-call(s32[1]{0:T(128)} %bitcast.core_ref, bf16[1024,512]{1,0:T(8,128)(2,1)S(1)} %get-tuple-element.172.normed_ref, bf16[1024,512]{1,0:T(8,128)(2,1)S(1)} %get-tuple-element.173.dquery, bf16[1024,512]{1,0:T(8,128)(2,1)S(1)} %get-tuple-element.174.dkey, ...), custom_call_target="tpu_custom_call" | custom-call | flops 3300000000 | bytes 1048576 | tf_op jit(solution)/shard_map/attention_weights/pallas_call | solution.py:520
  59.5 8.0 %wgrad2.1 = bf16[4608,256]{1,0:T(8,128)(2,1)S(1)} custom-call(s32[1]{0:T(128)} %bitcast.core_ref, f32[2,16]{1,0:T(2,128)S(1)} %broadcast_select_fusion.eq_ref, bf16[1024,256]{1,0:T(8,128)(2,1)} %copy-done.1, bf16[1024,256]{1,0:T(8,128)(2,1)} %copy-done.12, bf16[1024,512]{1,0:T(8,128)(2,1)} %get-tuple-element.191.refs_2_.refs_0_, ...), custom_call_target="tpu_custom_call" | custom-call | flops 7699999744 | bytes 1048576 | tf_op jit(solution)/shard_map/wgrad2/pallas_call | solution.py:565
  69.2 2.8 %collective-permute-start.14 = (bf16[2304,256]{1,0:T(8,128)(2,1)S(1)}, bf16[2304,256]{1,0:T(8,128)(2,1)S(1)}, u32[]{:S(2)}, u32[]{:S(2)}) collective-permute-start(bf16[2304,256]{1,0:T(8,128)(2,1)S(1)} %constant_dynamic-slice_fusion.15), channel_id=1, source_target_pairs={{0,8},{1,3},{2,10},{3,1},{4,12},{5,7},{6,14},{7,5},{8,0},{9,11},{1... | collective-permute-start | bytes 3538952 | tf_op jit(solution)/shard_map/ppermute | solution.py:711
  73.6 11.5 %dgrad2.1 = (bf16[1024,256]{1,0:T(8,128)(2,1)S(1)}, bf16[1024,256]{1,0:T(8,128)(2,1)S(1)}, f32[8,512]{1,0:T(8,128)S(1)}) custom-call(s32[1]{0:T(128)} %bitcast.core_ref, f32[16]{0:T(128)S(1)} %slice_bitcast_fusion.eq_ref, bf16[9,256,512]{2,1,0:T(8,128)(2,1)} %own_ref.1, bf16[9,256,512]{2,1,0:T(8,128)(2,1)} %copy-done.6, ...), custom_call_target="tpu_custom_call" | custom-call | flops 11000000512 | bytes 1048576 | tf_op jit(solution)/shard_map/dgrad2/pallas_call | solution.py:683
  90.2 8.2 %wgrad1.1 = (bf16[3072,256]{1,0:T(8,128)(2,1)S(1)}, bf16[1536,256]{1,0:T(8,128)(2,1)S(1)}) custom-call(s32[1]{0:T(128)} %bitcast.core_ref, f32[2,16]{1,0:T(2,128)S(1)} %broadcast_select_fusion.eq_ref, bf16[1024,256]{1,0:T(8,128)(2,1)} %copy-done.2, bf16[1024,256]{1,0:T(8,128)(2,1)} %copy-done.13, bf16[1024,256]{1,0:T(8,128)(2,1)} %get-tuple-element.180.refs_2_, ...), custom_call_target="tpu_custom_call" | custom-call | flops 7699999744 | bytes 1048576 | tf_op jit(solution)/shard_map/wgrad1/pallas_call | solution.py:613
  103.2 11.2 %dgrad1.1 = (f32[1024,256]{1,0:T(8,128)S(1)}, f32[1024,256]{1,0:T(8,128)S(1)}, f32[8,512]{1,0:T(8,128)S(1)}) custom-call(s32[1]{0:T(128)} %bitcast.core_ref, f32[16]{0:T(128)S(1)} %slice_bitcast_fusion.eq_ref, bf16[9,512,256]{2,1,0:T(8,128)(2,1)} %own_ref.2, bf16[9,512,256]{2,1,0:T(8,128)(2,1)} %copy-done.5, ...), custom_call_target="tpu_custom_call" | custom-call | flops 11000000512 | bytes 1048576 | tf_op jit(solution)/shard_map/dgrad1/pallas_call | solution.py:683
  116.8 2.6 %collective-permute-start.30 = (bf16[128,256]{1,0:T(8,128)(2,1)S(1)}, bf16[128,256]{1,0:T(8,128)(2,1)S(1)}, u32[]{:S(2)}, u32[]{:S(2)}) collective-permute-start(bf16[128,256]{1,0:T(8,128)(2,1)S(1)} %constant_dynamic-slice_fusion.4), channel_id=1, source_target_pairs={{0,16},{1,17},{2,18},{3,19},{4,20},{5,21},{6,22},{7,23},{8,24},{9,... | collective-permute-start | bytes 196616 | tf_op jit(solution)/shard_map/ppermute | solution.py:711
  120.4 2.9 %collective-permute-done.26 = f32[24,256]{1,0:T(8,128)S(1)} collective-permute-done((f32[24,256]{1,0:T(8,128)S(1)}, f32[24,256]{1,0:T(8,128)S(1)}, u32[]{:S(2)}, u32[]{:S(2)}) %collective-permute-start.26) | collective-permute-done | bytes 24608 | tf_op jit(solution)/shard_map/ppermute | solution.py:914
  124.0 3.0 %collective-permute-start.35 = (bf16[128,256]{1,0:T(8,128)(2,1)S(1)}, bf16[128,256]{1,0:T(8,128)(2,1)S(1)}, u32[]{:S(2)}, u32[]{:S(2)}) collective-permute-start(bf16[128,256]{1,0:T(8,128)(2,1)S(1)} %dynamic-slice_add_fusion.14), channel_id=1, source_target_pairs={{0,16},{1,17},{2,18},{3,19},{4,20},{5,21},{6,22},{7,23},{8,24},{9,... | collective-permute-start | bytes 196616 | tf_op jit(solution)/shard_map/ppermute | solution.py:711
  127.9 5.1 %collective-permute-start.27 = (bf16[768,256]{1,0:T(8,128)(2,1)S(1)}, bf16[768,256]{1,0:T(8,128)(2,1)S(1)}, u32[]{:S(2)}, u32[]{:S(2)}) collective-permute-start(bf16[768,256]{1,0:T(8,128)(2,1)S(1)} %constant_dynamic-slice_fusion.7), channel_id=1, source_target_pairs={{0,4},{1,3},{2,6},{3,1},{4,0},{5,7},{6,2},{7,5},{8,12},{9,11},{10,... | collective-permute-start | bytes 1179656 | tf_op jit(solution)/shard_map/ppermute | solution.py:711
  141.3 2.5 %collective-permute-start.38 = (bf16[96,256]{1,0:T(8,128)(2,1)S(1)}, bf16[96,256]{1,0:T(8,128)(2,1)S(1)}, u32[]{:S(2)}, u32[]{:S(2)}) collective-permute-start(bf16[96,256]{1,0:T(8,128)(2,1)S(1)} %constant_dynamic-slice_fusion), channel_id=1, source_target_pairs={{0,16},{1,17},{2,18},{3,19},{4,20},{5,21},{6,22},{7,23},{8,24},{9,... | collective-permute-start | bytes 147464 | tf_op jit(solution)/shard_map/ppermute | solution.py:711
  146.5 2.5 %collective-permute-done.38 = bf16[96,256]{1,0:T(8,128)(2,1)S(1)} collective-permute-done((bf16[96,256]{1,0:T(8,128)(2,1)S(1)}, bf16[96,256]{1,0:T(8,128)(2,1)S(1)}, u32[]{:S(2)}, u32[]{:S(2)}) %collective-permute-start.38) | collective-permute-done | bytes 49184 | tf_op jit(solution)/shard_map/ppermute | solution.py:711
  149.0 3.4 %collective-permute-start.42 = (bf16[96,256]{1,0:T(8,128)(2,1)S(1)}, bf16[96,256]{1,0:T(8,128)(2,1)S(1)}, u32[]{:S(2)}, u32[]{:S(2)}) collective-permute-start(bf16[96,256]{1,0:T(8,128)(2,1)S(1)} %dynamic-slice_add_fusion.15), channel_id=1, source_target_pairs={{0,16},{1,17},{2,18},{3,19},{4,20},{5,21},{6,22},{7,23},{8,24},{9,... | collective-permute-start | bytes 147464 | tf_op jit(solution)/shard_map/ppermute | solution.py:711
  152.4 2.7 %collective-permute-done.32 = bf16[384,256]{1,0:T(8,128)(2,1)S(1)} collective-permute-done((bf16[384,256]{1,0:T(8,128)(2,1)S(1)}, bf16[384,256]{1,0:T(8,128)(2,1)S(1)}, u32[]{:S(2)}, u32[]{:S(2)}) %collective-permute-start.32) | collective-permute-done | bytes 196640 | tf_op jit(solution)/shard_map/ppermute | solution.py:711
  157.7 5.2 %collective-permute-done.37 = bf16[192,256]{1,0:T(8,128)(2,1)S(1)} collective-permute-done((bf16[192,256]{1,0:T(8,128)(2,1)S(1)}, bf16[192,256]{1,0:T(8,128)(2,1)S(1)}, u32[]{:S(2)}, u32[]{:S(2)}) %collective-permute-start.37) | collective-permute-done | bytes 98336 | tf_op jit(solution)/shard_map/ppermute | solution.py:711
  163.8 4.6 %collective-permute-done.46 = bf16[192,256]{1,0:T(8,128)(2,1)S(1)} collective-permute-done((bf16[192,256]{1,0:T(8,128)(2,1)S(1)}, bf16[192,256]{1,0:T(8,128)(2,1)S(1)}, u32[]{:S(2)}, u32[]{:S(2)}) %collective-permute-start.46) | collective-permute-done | bytes 98336 | tf_op jit(solution)/shard_map/ppermute | solution.py:711
  170.8 5.6 %collective-permute-done.47 = bf16[384,256]{1,0:T(8,128)(2,1)} collective-permute-done((bf16[384,256]{1,0:T(8,128)(2,1)}, bf16[384,256]{1,0:T(8,128)(2,1)}, u32[]{:S(2)}, u32[]{:S(2)}) %collective-permute-start.47) | collective-permute-done | bytes 196640 | tf_op jit(solution)/shard_map/ppermute | solution.py:711
  182.0 7.6 %collective-permute-done.48 = bf16[768,256]{1,0:T(8,128)(2,1)S(1)} collective-permute-done((bf16[768,256]{1,0:T(8,128)(2,1)S(1)}, bf16[768,256]{1,0:T(8,128)(2,1)S(1)}, u32[]{:S(2)}, u32[]{:S(2)}) %collective-permute-start.48) | collective-permute-done | bytes 393248 | tf_op jit(solution)/shard_map/ppermute | solution.py:711
  198.5 2.8 %collective-permute-done.45.refs_0_ = bf16[768,256]{1,0:T(8,128)(2,1)S(1)} collective-permute-done((bf16[768,256]{1,0:T(8,128)(2,1)S(1)}, bf16[768,256]{1,0:T(8,128)(2,1)S(1)}, u32[]{:S(2)}, u32[]{:S(2)}) %collective-permute-start.45) | collective-permute-done | bytes 393248 | tf_op jit(solution)/shard_map/ppermute | solution.py:711
  201.3 3.0 %collective-permute-done.49.refs_1_ = bf16[1536,256]{1,0:T(8,128)(2,1)S(1)} collective-permute-done((bf16[1536,256]{1,0:T(8,128)(2,1)S(1)}, bf16[1536,256]{1,0:T(8,128)(2,1)S(1)}, u32[]{:S(2)}, u32[]{:S(2)}) %collective-permute-start.49) | collective-permute-done | bytes 786464 | tf_op jit(solution)/shard_map/ppermute | solution.py:711
  208.6 2.7 %place.2 = f32[2304,512]{1,0:T(8,128)} custom-call(s32[1]{0:T(128)} %bitcast.25.base_ref, bf16[2304,256]{1,0:T(8,128)(2,1)S(1)} %pad_maximum_fusion.refs_0_, bf16[2304,256]{1,0:T(8,128)(2,1)S(1)} %collective-permute-done.51.refs_1_), custom_call_target="tpu_custom_call" | custom-call | flops 2200000000 | bytes 1048576 | tf_op jit(solution)/shard_map/place/pallas_call | solution.py:819
  (199 shorter events, 63.5 us)
Async XLA Ops:
  17.5 36.4 %collective-permute-start.11 = (bf16[1024,256]{1,0:T(8,128)(2,1)}, bf16[1024,256]{1,0:T(8,128)(2,1)S(1)}, u32[]{:S(2)}, u32[]{:S(2)}) collective-permute-start(bf16[1024,256]{1,0:T(8,128)(2,1)} %get-tuple-element.179.refs_3_), channel_id=1, source_target_pairs={{0,1},{1,0},{2,3},{3,2},{4,5},{5,4},{6,7},{7,6},{8,9},{9,8},{10,11... | collective-permute-start | bytes 1572872 | tf_op jit(solution)/shard_map/ppermute | solution.py:828
  17.8 36.1 %collective-permute-start.12 = (bf16[1024,256]{1,0:T(8,128)(2,1)}, bf16[1024,256]{1,0:T(8,128)(2,1)S(1)}, u32[]{:S(2)}, u32[]{:S(2)}) collective-permute-start(bf16[1024,256]{1,0:T(8,128)(2,1)} %get-tuple-element.180.refs_2_), channel_id=1, source_target_pairs={{0,1},{1,0},{2,3},{3,2},{4,5},{5,4},{6,7},{7,6},{8,9},{9,8},{10,11... | collective-permute-start | bytes 1572872 | tf_op jit(solution)/shard_map/ppermute | solution.py:828
  25.0 28.9 %collective-permute-start.10 = (bf16[1024,256]{1,0:T(8,128)(2,1)S(1)}, bf16[1024,256]{1,0:T(8,128)(2,1)S(1)}, u32[]{:S(2)}, u32[]{:S(2)}) collective-permute-start(bf16[1024,256]{1,0:T(8,128)(2,1)S(1)} %get-tuple-element.164.act_peer), channel_id=1, source_target_pairs={{0,1},{1,0},{2,3},{3,2},{4,5},{5,4},{6,7},{7,6},{8,9},{9,8},{10,11... | collective-permute-start | bytes 1572872 | tf_op jit(solution)/shard_map/ppermute | solution.py:828
  69.2 17.0 %collective-permute-start.14 = (bf16[2304,256]{1,0:T(8,128)(2,1)S(1)}, bf16[2304,256]{1,0:T(8,128)(2,1)S(1)}, u32[]{:S(2)}, u32[]{:S(2)}) collective-permute-start(bf16[2304,256]{1,0:T(8,128)(2,1)S(1)} %constant_dynamic-slice_fusion.15), channel_id=1, source_target_pairs={{0,8},{1,3},{2,10},{3,1},{4,12},{5,7},{6,14},{7,5},{8,0},{9,11},{1... | collective-permute-start | bytes 3538952 | tf_op jit(solution)/shard_map/ppermute | solution.py:711
  72.0 13.9 %collective-permute-start.15 = (bf16[1024,256]{1,0:T(8,128)(2,1)S(1)}, bf16[1024,256]{1,0:T(8,128)(2,1)S(1)}, u32[]{:S(2)}, u32[]{:S(2)}) collective-permute-start(bf16[1024,256]{1,0:T(8,128)(2,1)S(1)} %constant_dynamic-slice_fusion.14), channel_id=1, source_target_pairs={{0,4},{1,5},{2,6},{3,7},{4,0},{5,1},{6,2},{7,3},{8,12},{9,13},{10,... | collective-permute-start | bytes 1572872 | tf_op jit(solution)/shard_map/ppermute | solution.py:711
  98.8 15.7 %collective-permute-start.19 = (bf16[256,256]{1,0:T(8,128)(2,1)S(1)}, bf16[256,256]{1,0:T(8,128)(2,1)S(1)}, u32[]{:S(2)}, u32[]{:S(2)}) collective-permute-start(bf16[256,256]{1,0:T(8,128)(2,1)S(1)} %constant_dynamic-slice_fusion.11), channel_id=1, source_target_pairs={{0,2},{1,3},{2,0},{3,1},{4,6},{5,7},{6,4},{7,5},{8,10},{9,11},{10,... | collective-permute-start | bytes 393224 | tf_op jit(solution)/shard_map/ppermute | solution.py:711
  99.6 14.9 %collective-permute-start.20 = (bf16[576,256]{1,0:T(8,128)(2,1)S(1)}, bf16[576,256]{1,0:T(8,128)(2,1)S(1)}, u32[]{:S(2)}, u32[]{:S(2)}) collective-permute-start(bf16[576,256]{1,0:T(8,128)(2,1)S(1)} %constant_dynamic-slice_fusion.10), channel_id=1, source_target_pairs={{0,4},{1,9},{2,6},{3,11},{4,0},{5,13},{6,2},{7,15},{8,12},{9,1},{1... | collective-permute-start | bytes 884744 | tf_op jit(solution)/shard_map/ppermute | solution.py:711
  101.0 13.6 %collective-permute-start.21 = (bf16[768,256]{1,0:T(8,128)(2,1)S(1)}, bf16[768,256]{1,0:T(8,128)(2,1)S(1)}, u32[]{:S(2)}, u32[]{:S(2)}) collective-permute-start(bf16[768,256]{1,0:T(8,128)(2,1)S(1)} %constant_dynamic-slice_fusion.9), channel_id=1, source_target_pairs={{0,4},{1,5},{2,6},{3,7},{4,0},{5,1},{6,2},{7,3},{8,12},{9,13},{10,... | collective-permute-start | bytes 1179656 | tf_op jit(solution)/shard_map/ppermute | solution.py:711
  101.9 12.9 %collective-permute-start.22 = (bf16[1536,256]{1,0:T(8,128)(2,1)S(1)}, bf16[1536,256]{1,0:T(8,128)(2,1)S(1)}, u32[]{:S(2)}, u32[]{:S(2)}) collective-permute-start(bf16[1536,256]{1,0:T(8,128)(2,1)S(1)} %constant_dynamic-slice_fusion.8), channel_id=1, source_target_pairs={{0,2},{1,9},{2,0},{3,11},{4,6},{5,13},{6,4},{7,15},{8,10},{9,1},{1... | collective-permute-start | bytes 2359304 | tf_op jit(solution)/shard_map/ppermute | solution.py:711
  115.4 20.8 %collective-permute-start.28 = (bf16[384,256]{1,0:T(8,128)(2,1)S(1)}, bf16[384,256]{1,0:T(8,128)(2,1)S(1)}, u32[]{:S(2)}, u32[]{:S(2)}) collective-permute-start(bf16[384,256]{1,0:T(8,128)(2,1)S(1)} %constant_dynamic-slice_fusion.6), channel_id=1, source_target_pairs={{0,8},{1,9},{2,10},{3,11},{4,12},{5,13},{6,14},{7,15},{8,0},{9,1},... | collective-permute-start | bytes 589832 | tf_op jit(solution)/shard_map/ppermute | solution.py:711
  120.0 15.8 %collective-permute-start.29 = (bf16[288,256]{1,0:T(8,128)(2,1)S(1)}, bf16[288,256]{1,0:T(8,128)(2,1)S(1)}, u32[]{:S(2)}, u32[]{:S(2)}) collective-permute-start(bf16[288,256]{1,0:T(8,128)(2,1)S(1)} %constant_dynamic-slice_fusion.5), channel_id=1, source_target_pairs={{0,16},{1,17},{2,18},{3,19},{4,20},{5,21},{6,22},{7,23},{8,24},{9,... | collective-permute-start | bytes 442376 | tf_op jit(solution)/shard_map/ppermute | solution.py:711
  127.9 17.1 %collective-permute-start.27 = (bf16[768,256]{1,0:T(8,128)(2,1)S(1)}, bf16[768,256]{1,0:T(8,128)(2,1)S(1)}, u32[]{:S(2)}, u32[]{:S(2)}) collective-permute-start(bf16[768,256]{1,0:T(8,128)(2,1)S(1)} %constant_dynamic-slice_fusion.7), channel_id=1, source_target_pairs={{0,4},{1,3},{2,6},{3,1},{4,0},{5,7},{6,2},{7,5},{8,12},{9,11},{10,... | collective-permute-start | bytes 1179656 | tf_op jit(solution)/shard_map/ppermute | solution.py:711
  133.0 36.2 %collective-permute-start.41 = (f32[24,256]{1,0:T(8,128)S(1)}, f32[24,256]{1,0:T(8,128)S(1)}, u32[]{:S(2)}, u32[]{:S(2)}) collective-permute-start(f32[24,256]{1,0:T(8,128)S(1)} %add.244), channel_id=1, source_target_pairs={{0,16},{2,18},{4,20},{6,22},{8,24},{10,26},{12,28},{14,30},{16,0},... | collective-permute-start | bytes 73736 | tf_op jit(solution)/shard_map/ppermute | solution.py:914
  139.6 37.9 %collective-permute-start.52 = (bf16[512,256]{1,0:T(8,128)(2,1)S(1)}, bf16[512,256]{1,0:T(8,128)(2,1)}, u32[]{:S(2)}, u32[]{:S(2)}) collective-permute-start(bf16[512,256]{1,0:T(8,128)(2,1)S(1)} %pad_maximum_fusion.7), channel_id=1, source_target_pairs={{0,8},{1,9},{2,10},{3,11},{4,12},{5,13},{6,14},{7,15},{8,0},{9,1},... | collective-permute-start | bytes 786440 | tf_op jit(solution)/shard_map/ppermute | solution.py:711
  143.8 19.1 %collective-permute-start.39 = (bf16[576,256]{1,0:T(8,128)(2,1)S(1)}, bf16[576,256]{1,0:T(8,128)(2,1)S(1)}, u32[]{:S(2)}, u32[]{:S(2)}) collective-permute-start(bf16[576,256]{1,0:T(8,128)(2,1)S(1)} %pad_maximum_fusion.6), channel_id=1, source_target_pairs={{0,4},{1,9},{2,6},{3,11},{4,0},{5,13},{6,2},{7,15},{8,12},{9,1},{1... | collective-permute-start | bytes 884744 | tf_op jit(solution)/shard_map/ppermute | solution.py:711
  156.8 12.5 %collective-permute-start.43 = (bf16[192,256]{1,0:T(8,128)(2,1)}, bf16[192,256]{1,0:T(8,128)(2,1)}, u32[]{:S(2)}, u32[]{:S(2)}) collective-permute-start(bf16[192,256]{1,0:T(8,128)(2,1)} %pad_maximum_fusion.11), channel_id=1, source_target_pairs={{0,2},{1,3},{2,0},{3,1},{4,6},{5,7},{6,4},{7,5},{8,10},{9,11},{10,... | collective-permute-start | bytes 294920 | tf_op jit(solution)/shard_map/ppermute | solution.py:711
  163.8 14.8 %collective-permute-start.50 = (bf16[1152,256]{1,0:T(8,128)(2,1)}, bf16[1152,256]{1,0:T(8,128)(2,1)}, u32[]{:S(2)}, u32[]{:S(2)}) collective-permute-start(bf16[1152,256]{1,0:T(8,128)(2,1)} %pad_maximum_fusion.2), channel_id=1, source_target_pairs={{0,2},{1,5},{2,0},{3,7},{4,6},{5,1},{6,4},{7,3},{8,10},{9,13},{10,... | collective-permute-start | bytes 1769480 | tf_op jit(solution)/shard_map/ppermute | solution.py:711
  169.2 22.4 %collective-permute-start.23 = (f32[1024,256]{1,0:T(8,128)S(1)}, f32[1024,256]{1,0:T(8,128)S(1)}, u32[]{:S(2)}, u32[]{:S(2)}) collective-permute-start(f32[1024,256]{1,0:T(8,128)S(1)} %get-tuple-element.219), channel_id=1, source_target_pairs={{0,1},{1,0},{2,3},{3,2},{4,5},{5,4},{6,7},{7,6},{8,9},{9,8},{10,11... | collective-permute-start | bytes 3145736 | tf_op jit(solution)/shard_map/ppermute | solution.py:828
  169.3 24.2 %collective-permute-start.24 = (f32[1024,256]{1,0:T(8,128)}, f32[1024,256]{1,0:T(8,128)S(1)}, u32[]{:S(2)}, u32[]{:S(2)}) collective-permute-start(f32[1024,256]{1,0:T(8,128)} %copy-done), channel_id=1, source_target_pairs={{0,1},{1,0},{2,3},{3,2},{4,5},{5,4},{6,7},{7,6},{8,9},{9,8},{10,11... | collective-permute-start | bytes 3145736 | tf_op jit(solution)/shard_map/ppermute | solution.py:828
  176.4 13.2 %collective-permute-start.44 = (bf16[384,256]{1,0:T(8,128)(2,1)S(1)}, bf16[384,256]{1,0:T(8,128)(2,1)S(1)}, u32[]{:S(2)}, u32[]{:S(2)}) collective-permute-start(bf16[384,256]{1,0:T(8,128)(2,1)S(1)} %pad_maximum_fusion.8), channel_id=1, source_target_pairs={{0,8},{1,9},{2,10},{3,11},{4,12},{5,13},{6,14},{7,15},{8,0},{9,1},... | collective-permute-start | bytes 589832 | tf_op jit(solution)/shard_map/ppermute | solution.py:711
  177.5 12.1 %collective-permute-start.48 = (bf16[768,256]{1,0:T(8,128)(2,1)S(1)}, bf16[768,256]{1,0:T(8,128)(2,1)S(1)}, u32[]{:S(2)}, u32[]{:S(2)}) collective-permute-start(bf16[768,256]{1,0:T(8,128)(2,1)S(1)} %pad_maximum_fusion.5), channel_id=1, source_target_pairs={{0,4},{1,3},{2,6},{3,1},{4,0},{5,7},{6,2},{7,5},{8,12},{9,11},{10,... | collective-permute-start | bytes 1179656 | tf_op jit(solution)/shard_map/ppermute | solution.py:711
  178.6 18.5 %collective-permute-start.53 = (bf16[1024,256]{1,0:T(8,128)(2,1)S(1)}, bf16[1024,256]{1,0:T(8,128)(2,1)S(1)}, u32[]{:S(2)}, u32[]{:S(2)}) collective-permute-start(bf16[1024,256]{1,0:T(8,128)(2,1)S(1)} %pad_maximum_fusion.3.refs_0_), channel_id=1, source_target_pairs={{0,4},{1,5},{2,6},{3,7},{4,0},{5,1},{6,2},{7,3},{8,12},{9,13},{10,... | collective-permute-start | bytes 1572872 | tf_op jit(solution)/shard_map/ppermute | solution.py:711
  189.6 19.0 %collective-permute-start.51 = (bf16[2304,256]{1,0:T(8,128)(2,1)S(1)}, bf16[2304,256]{1,0:T(8,128)(2,1)S(1)}, u32[]{:S(2)}, u32[]{:S(2)}) collective-permute-start(bf16[2304,256]{1,0:T(8,128)(2,1)S(1)} %pad_maximum_fusion.refs_0_), channel_id=1, source_target_pairs={{0,8},{1,3},{2,10},{3,1},{4,12},{5,7},{6,14},{7,5},{8,0},{9,11},{1... | collective-permute-start | bytes 3538952 | tf_op jit(solution)/shard_map/ppermute | solution.py:711
  189.7 14.6 %collective-permute-start.49 = (bf16[1536,256]{1,0:T(8,128)(2,1)S(1)}, bf16[1536,256]{1,0:T(8,128)(2,1)S(1)}, u32[]{:S(2)}, u32[]{:S(2)}) collective-permute-start(bf16[1536,256]{1,0:T(8,128)(2,1)S(1)} %pad_maximum_fusion.1.refs_1_), channel_id=1, source_target_pairs={{0,2},{1,9},{2,0},{3,11},{4,6},{5,13},{6,4},{7,15},{8,10},{9,1},{1... | collective-permute-start | bytes 2359304 | tf_op jit(solution)/shard_map/ppermute | solution.py:711
  (48 other events, 308.5 us)
